TPU v7x, 32 devices: a whole 2x2x4 slice. The times are simulated.
32 devices in a mesh: dp: 8 (over z, x), lat: 4 (over y, core).
Axes of the slice: x: 2, y: 2, z: 4, core: 2. Of those that a mesh axis runs over, the one named last changes fastest.
Arguments:
- tokens: bfloat16 [24576, 512], P(('dp', 'lat')), may hold values from -6 to 6
- latents: bfloat16 [1536, 1024], P(('dp', 'lat')), may hold values from -6 to 6
- gain_self: float32 [512], replicated, may hold values from 0.1 to 1.9
- w_qkv_tok: bfloat16 [512, 1536], replicated, may hold values from -1 to 1
- w_o_tok: bfloat16 [512, 512], replicated, may hold values from -0.25 to 0.25
- gain_read: float32 [512], replicated, may hold values from 0.1 to 1.9
- w_kv_read: bfloat16 [512, 2048], replicated, may hold values from -1 to 1
- gain_lat: float32 [1024], replicated, may hold values from 0.1 to 1.9
- w_q_read: bfloat16 [1024, 1024], replicated, may hold values from -1 to 1
- gain_glob: float32 [1024], replicated, may hold values from 0.1 to 1.9
- w_qkv_glob: bfloat16 [3, 1024, 1024], P(None, None, 'lat'), may hold values from -1 to 1
- w_o_glob: bfloat16 [1024, 1024], P('lat'), may hold values from -0.375 to 0.375
- gain_write: float32 [512], replicated, may hold values from 0.1 to 1.9
- w_q_write: bfloat16 [512, 512], replicated, may hold values from -1 to 1
- gain_wlat: float32 [1024], replicated, may hold values from 0.1 to 1.9
- w_kv_write: bfloat16 [1024, 1024], replicated, may hold values from -1 to 1
Outputs:
- tokens_out: bfloat16 [24576, 512], P(('dp', 'lat'))
- latents_out: bfloat16 [1536, 1024], P(('dp', 'lat'))
All inputs are finite; a program needn't handle non-finite values.
Results may differ from a plain program's by a relative error of at most 0.015.
Values may be sent and summed in bfloat16 or wider, within the bound.
A program may use at most 128 MiB of HBM per device.

v0:
```python
import functools

import jax
import jax.numpy as jnp
from jax import lax
from jax.experimental import pallas as pl
from jax.experimental.pallas import tpu as pltpu
from jax.sharding import PartitionSpec as P

HEAD = 64
G = 256
NLAT = 16
SCALE = HEAD ** (-0.5)
MESH = pl.DeviceIdType.MESH
PARTS = 4
F32 = jnp.float32
BF16 = jnp.bfloat16


def rms_norm(values, gain):
    floats = values.astype(F32)
    factor = lax.rsqrt(jnp.mean(floats * floats, axis=-1, keepdims=True) + 1e-06)
    return (floats * factor * gain).astype(BF16)


def dot(a, b):
    return jnp.dot(a, b, preferred_element_type=F32)


def dot_nt(a, b):
    return lax.dot_general(a, b, (((1,), (1,)), ((), ())), preferred_element_type=F32)


def dot_tn(a, b):
    return lax.dot_general(a, b, (((0,), (0,)), ((), ())), preferred_element_type=F32)


def spread_heads(query, count):
    lane_head = lax.broadcasted_iota(jnp.int32, query.shape, 1) // HEAD
    zero = jnp.zeros_like(query)
    return jnp.concatenate([jnp.where(lane_head == h, query, zero) for h in range(count)], axis=0)


def fold_heads(stacked, count):
    rows = stacked.shape[0] // count
    lane_head = lax.broadcasted_iota(jnp.int32, (rows, stacked.shape[1]), 1) // HEAD
    out = stacked[:rows]
    for h in range(1, count):
        out = jnp.where(lane_head == h, stacked[h * rows : (h + 1) * rows], out)
    return out


def softmax_mix(stacked, keys, values):
    scores = dot_nt(stacked, keys)
    peak = jnp.max(scores, axis=-1, keepdims=True)
    weights = jnp.exp(scores - peak)
    total = jnp.sum(weights, axis=-1, keepdims=True)
    return dot(weights.astype(BF16), values) * (1.0 / total)


def kernel(
    dp_count,
    lat_count,
    tok,
    lat_in,
    g_self,
    w_qkv_h,
    w_o_h,
    g_read,
    w_kvr_h,
    g_lat,
    w_qr_h,
    g_glob,
    w_glob_h,
    w_og_h,
    g_write,
    w_qw_h,
    g_wlat,
    w_kvw_h,
    tok_out,
    lat_out,
    mid,
    lfin,
    w_qkv,
    w_o,
    w_kvr,
    w_qr,
    w_glob,
    w_og,
    w_qw,
    w_kvw,
    lmid,
    rq,
    packed,
    mixed,
    kvr,
    gath,
    kv,
    qq,
    msend,
    mrecv,
    top,
    norm,
    acc,
    load_sem,
    z_send,
    z_recv,
    f_send,
    f_recv,
    s_send,
    s_recv,
    c_send,
    c_recv,
    wo_send,
    wo_recv,
    m_send,
    m_recv,
):
    width = tok.shape[1]
    lat_width = lat_in.shape[1]
    groups = tok.shape[0] // G
    lat_rows = lat_in.shape[0]
    nz = dp_count // 2
    dp = lax.axis_index("dp")
    lat = lax.axis_index("lat")
    z, x = dp // 2, dp % 2
    y, core = lat // 2, lat % 2
    dp_x = dp + 1 - 2 * x
    lat_y = (lat + 2) % 4
    partner = lat + 1 - 2 * core
    diag = (partner + 2) % 4
    a = (1 - core) * y + core * x
    b = (1 - core) * x + core * y
    first = ((1 - core) * dp + core * dp_x, (1 - core) * lat_y + core * lat)
    second = ((1 - core) * dp_x + core * dp, (1 - core) * lat + core * lat_y)
    base = (b * 2 + a) * nz
    other = (b * 2 + 1 - a) * nz
    me = base + z
    far = (1 - 2 * b) * 2 * nz
    run = nz // PARTS

    loads = []
    for i, (src, dst) in enumerate(
        ((w_qkv_h, w_qkv), (w_o_h, w_o), (w_qr_h, w_qr), (w_kvr_h, w_kvr), (w_glob_h, w_glob),
         (w_qw_h, w_qw), (w_kvw_h, w_kvw), (w_og_h, w_og.at[lat]))
    ):
        loads.append(pltpu.make_async_copy(src, dst, load_sem.at[i]))
        loads[-1].start()

    barrier = pltpu.get_barrier_semaphore()

    def greet(offset, carry):
        pl.semaphore_signal(
            barrier, inc=1, device_id=((z + offset) % nz * 2 + x, lat), device_id_type=MESH
        )
        return carry

    lax.fori_loop(1, nz, greet, 0)
    for peer in ((dp_x, lat), (dp, lat_y), (dp, partner), (dp, diag)):
        pl.semaphore_signal(barrier, inc=1, device_id=peer, device_id_type=MESH)
    pl.semaphore_wait(barrier, nz + 3)

    def remote(src, dst, send_sem, recv_sem, peer):
        return pltpu.make_async_remote_copy(
            src_ref=src, dst_ref=dst, send_sem=send_sem, recv_sem=recv_sem, device_id=peer,
            device_id_type=MESH,
        )

    wo_first = [
        remote(w_og_h, w_og.at[lat], wo_send.at[0], wo_recv.at[0], (dp, partner)),
        remote(w_og_h, w_og.at[lat], wo_send.at[1], wo_recv.at[1], (dp, lat_y)),
    ]
    wo_relay = remote(w_og.at[lat_y], w_og.at[lat_y], wo_send.at[2], wo_recv.at[2], (dp, partner))
    for copy in wo_first:
        copy.start()

    def piece(g, start, count):
        return gath.at[g, core, pl.ds(start, count)]

    def along(ref, send_sem, recv_sem, peer):
        return remote(ref, ref, send_sem, recv_sem, peer)

    def on_first(g, p):
        return along(
            piece(g, base + p * run, run), f_send.at[g, p], f_recv.at[g, p], first
        )

    def on_second(g, half, p):
        start = base + (other - base) * half + p * run
        k = half * PARTS + p
        return along(piece(g, start, run), s_send.at[g, k], s_recv.at[g, k], second)

    def share(g, line, p):
        start = (base, other, base + far, other + far)[line] + p * run
        k = line * PARTS + p
        return along(
            piece(g, start, run), c_send.at[g, k], c_recv.at[g, k], (dp, partner)
        )

    def z_copy(g, offset):
        return remote(
            gath.at[g, core, me], gath.at[g, core, me], z_send.at[g, (z + offset) % nz],
            z_recv.at[g, z], ((z + offset) % nz * 2 + x, lat),
        )

    def each(low, high, body):
        def one(i, carry):
            body(i)
            return carry

        lax.fori_loop(low, high, one, 0)

    def z_start(g):
        each(1, nz, lambda offset: z_copy(g, offset).start())

    def z_arrived(g, block):
        ref = piece(g, base + block, 1)

        @pl.when(block != z)
        def _():
            pltpu.make_async_copy(ref, ref, z_recv.at[g, block]).wait()

    def stage_one(g, low, high):
        def body(o):
            p = (z // run + o) % PARTS
            each(0, run, lambda i: z_arrived(g, p * run + i))
            on_first(g, p).start()
            on_second(g, 0, p).start()
            share(g, 0, p).start()

        each(low, high, body)

    def stage_two(g):
        def body(o):
            p = (z // run + o) % PARTS
            on_first(g, p).wait_recv()
            on_second(g, 1, p).start()
            share(g, 1, p).start()

        each(0, PARTS, body)

    def second_arrived(g, half, o):
        p = (z // run + o) % PARTS
        on_second(g, half, p).wait_recv()
        share(g, 2 + half, p).start()

    def stage_three(g):
        for half in range(2):
            each(0, PARTS, lambda o: second_arrived(g, half, o))

    def gathered(g):
        for line in range(4):
            each(0, PARTS, lambda p: share(g, line, p).wait_recv())

    def self_part(g):
        rows = pl.ds(g * G, G)
        group = tok[rows, :]
        normed = rms_norm(group, g_self[...])
        if g == 0:
            loads[0].wait()
        packed[...] = dot(normed, w_qkv[...]).astype(BF16)
        for pair in range(width // (2 * HEAD)):
            at = pair * 2 * HEAD
            query = packed[:, at : at + 2 * HEAD] * jnp.asarray(SCALE, BF16)
            keys = packed[:, width + at : width + at + 2 * HEAD]
            values = packed[:, 2 * width + at : 2 * width + at + 2 * HEAD]
            out = softmax_mix(spread_heads(query, 2), keys, values)
            mixed[:, at : at + 2 * HEAD] = fold_heads(out, 2).astype(BF16)
        if g == 0:
            loads[1].wait()
        mid[rows, :] = (group.astype(F32) + dot(mixed[...], w_o[...])).astype(BF16)

    def read_part(g):
        if g == 0:
            loads[2].wait()
            query = dot(rms_norm(lat_in[...], g_lat[...]), w_qr[...]).astype(BF16)
            rq[...] = query * jnp.asarray(SCALE, BF16)
            loads[3].wait()
        rows = pl.ds(g * G, G)
        lrows = pl.ds(g * NLAT, NLAT)
        kvr[...] = dot(rms_norm(mid[rows, :], g_read[...]), w_kvr[...]).astype(BF16)
        quad = 4 * HEAD
        for at in range(0, lat_width, quad):
            out = softmax_mix(
                spread_heads(rq[lrows, at : at + quad], 4),
                kvr[:, at : at + quad],
                kvr[:, lat_width + at : lat_width + at + quad],
            )
            lmid[lrows, at : at + quad] = (
                lat_in[lrows, at : at + quad].astype(F32) + fold_heads(out, 4)
            ).astype(BF16)
        gath[g, core, me] = rms_norm(lmid[lrows, :], g_glob[...])
        z_start(g)
        stage_one(g, 0, 1)

    last = groups - 1
    for g in range(groups):
        self_part(g)
        if g >= 2:
            stage_one(g - 2, 1, PARTS)
            if g == 2:
                wo_first[1].wait_recv()
                wo_relay.start()
        read_part(g)

    block_rows = 4 * nz * NLAT
    tile = min(block_rows, G)
    blocks = tile // NLAT

    def project(g, c):
        def one(i, carry):
            rows = gath[g, c, pl.ds(i * blocks, blocks)].reshape(tile, lat_width)
            at = pl.multiple_of((g * 2 + c) * block_rows + i * tile, tile)
            kv[0, pl.ds(at, tile), :] = dot(rows, w_glob[1]).astype(BF16)
            kv[1, pl.ds(at, tile), :] = dot(rows, w_glob[2]).astype(BF16)
            return carry

        lax.fori_loop(0, block_rows // tile, one, 0)

    for g in range(last - 1):
        stage_two(g)
    loads[5].wait()
    for g in range(groups):
        rows = pl.ds(g * G, G)
        query = dot(rms_norm(mid[rows, :], g_write[...]), w_qw[...]).astype(BF16)
        tok_out[rows, :] = query * jnp.asarray(SCALE, BF16)
    stage_one(last - 1, 1, PARTS)
    loads[4].wait()
    for g in range(last - 1):
        stage_three(g)
    stage_two(last - 1)
    for g in range(last - 1):
        gathered(g)
        project(g, 0)
        project(g, 1)
    stage_one(last, 1, PARTS)
    stage_two(last)
    stage_three(last - 1)
    gathered(last - 1)
    project(last - 1, 0)
    project(last - 1, 1)
    own_p = z // run

    @pl.when(core == 1)
    def _():
        on_second(last, 0, own_p).wait_recv()
        share(last, 2, own_p).start()
        for line in range(2):
            share(last, line, own_p).wait_recv()

    @pl.when(core == 0)
    def _():
        for line in (0, 2):
            share(last, line, own_p).wait_recv()

    own = []
    for l in range(lat_count):
        ly, lc = l // 2, l % 2
        index = ((x * 2 + ly) if lc == 0 else (ly * 2 + x)) * nz + z
        for g in range(groups):
            own.append(gath[g, lc, index])
    query = dot(jnp.concatenate(own, axis=0), w_glob[0]).astype(BF16) * jnp.asarray(SCALE, BF16)
    heads = query.shape[1] // HEAD
    qq[...] = spread_heads(query, heads)
    early = last * 2 * block_rows
    full = lat_rows * lat_count
    part = full if early * full <= 2**20 else lat_rows

    def attend_early(i, carry):
        rows = pl.ds(pl.multiple_of(i * part, part), part)
        scores = dot_nt(qq[rows, :], kv[0, :early, :])
        peak = jnp.max(scores, axis=-1, keepdims=True)
        weights = jnp.exp(scores - peak)
        top[rows, :] = peak
        norm[rows, :] = jnp.sum(weights, axis=-1, keepdims=True)
        acc[rows, :] = dot(weights.astype(BF16), kv[1, :early, :])
        return carry

    def attend_late(i, carry):
        rows = pl.ds(pl.multiple_of(i * part, part), part)
        scores = dot_nt(qq[rows, :], kv[0, early:, :])
        peak = jnp.maximum(top[rows, :], jnp.max(scores, axis=-1, keepdims=True))
        weights = jnp.exp(scores - peak)
        keep = jnp.exp(top[rows, :] - peak)
        total = norm[rows, :] * keep + jnp.sum(weights, axis=-1, keepdims=True)
        both = acc[rows, :] * keep + dot(weights.astype(BF16), kv[1, early:, :])
        qq[rows, :] = (both * (1.0 / total)).astype(BF16)
        return carry

    lax.fori_loop(0, qq.shape[0] // part, attend_early, 0)

    @pl.when(core == 1)
    def _():
        each(1, PARTS, lambda o: second_arrived(last, 0, o))
        each(0, PARTS, lambda o: second_arrived(last, 1, o))
        for line in range(2):
            each(1, PARTS, lambda o: share(last, line, (own_p + o) % PARTS).wait_recv())
        for line in range(2, 4):
            each(0, PARTS, lambda p: share(last, line, p).wait_recv())

    @pl.when(core == 0)
    def _():
        stage_three(last)
        for line in (0, 2):
            each(1, PARTS, lambda o: share(last, line, (own_p + o) % PARTS).wait_recv())
        for line in (1, 3):
            each(0, PARTS, lambda p: share(last, line, p).wait_recv())

    project(last, 0)
    project(last, 1)
    lax.fori_loop(0, qq.shape[0] // part, attend_late, 0)
    result = fold_heads(qq[...], heads)
    for l in range(lat_count):
        msend[l] = result[l * lat_rows : (l + 1) * lat_rows]
    mix_copies = []
    for i, peer in enumerate((partner, lat_y, diag)):
        mix_copies.append(remote(msend.at[peer], mrecv.at[lat], m_send.at[i], m_recv.at[i], (dp, peer)))
        mix_copies[-1].start()
    mrecv[lat] = msend[lat]
    loads[7].wait()
    loads[6].wait()
    wo_first[0].wait_recv()
    wo_relay.wait_recv()
    for copy in mix_copies:
        copy.wait_recv()
    total = dot(mrecv[0], w_og[0])
    for l in range(1, lat_count):
        total = total + dot(mrecv[l], w_og[l])
    final = (lmid[...].astype(F32) + total).astype(BF16)
    lat_out[...] = final
    lfin[...] = dot(rms_norm(final, g_wlat[...]), w_kvw[...]).astype(BF16)

    for copy in wo_first + [wo_relay] + mix_copies:
        copy.wait_send()
    for g in range(groups):
        each(1, nz, lambda offset: z_copy(g, offset).wait_send())

        def sent(p):
            on_first(g, p).wait_send()
            for half in range(2):
                on_second(g, half, p).wait_send()
            for line in range(4):
                share(g, line, p).wait_send()

        each(0, PARTS, sent)


def back(query, final, mid, key_vals, tok_out, lat_out):
    width = query.shape[1]
    heads = width // HEAD
    keys = spread_heads(key_vals[:, :width], heads)
    values = spread_heads(key_vals[:, width:], heads)
    scores = dot_nt(keys, query[...]).reshape(heads, NLAT, G)
    peak = jnp.max(scores, axis=1, keepdims=True)
    weights = jnp.exp(scores - peak)
    weights = weights * (1.0 / jnp.sum(weights, axis=1, keepdims=True))
    written = dot_tn(weights.reshape(heads * NLAT, G).astype(BF16), values)
    tok_out[...] = (mid[...].astype(F32) + written).astype(BF16)
    lat_out[...] = final[...]


def local(
    tokens, latents, gain_self, w_qkv_tok, w_o_tok, gain_read, w_kv_read, gain_lat, w_q_read,
    gain_glob, w_qkv_glob, w_o_glob, gain_write, w_q_write, gain_wlat, w_kv_write,
):
    dp_count = lax.axis_size("dp")
    lat_count = lax.axis_size("lat")
    rows, width = tokens.shape
    lat_rows, lat_width = latents.shape
    groups = rows // G
    here = w_qkv_glob.shape[2]
    nz = dp_count // 2
    all_rows = lat_rows * dp_count * lat_count
    vmem = pl.BlockSpec(memory_space=pltpu.VMEM)
    hbm = pl.BlockSpec(memory_space=pl.ANY)
    dma = pltpu.SemaphoreType.DMA
    query, final, mid, key_vals = pl.pallas_call(
        functools.partial(kernel, dp_count, lat_count),
        out_shape=(
            jax.ShapeDtypeStruct(tokens.shape, BF16),
            jax.ShapeDtypeStruct(latents.shape, BF16),
            jax.ShapeDtypeStruct(tokens.shape, BF16),
            jax.ShapeDtypeStruct((lat_rows, w_kv_write.shape[1]), BF16),
        ),
        in_specs=[vmem, vmem, vmem, hbm, hbm, vmem, hbm, vmem, hbm, vmem, hbm, hbm, vmem, hbm, vmem, hbm],
        out_specs=(vmem,) * 4,
        scratch_shapes=[
            pltpu.VMEM(w_qkv_tok.shape, BF16),
            pltpu.VMEM(w_o_tok.shape, BF16),
            pltpu.VMEM(w_kv_read.shape, BF16),
            pltpu.VMEM(w_q_read.shape, BF16),
            pltpu.VMEM(w_qkv_glob.shape, BF16),
            pltpu.VMEM((lat_count,) + w_o_glob.shape, BF16),
            pltpu.VMEM(w_q_write.shape, BF16),
            pltpu.VMEM(w_kv_write.shape, BF16),
            pltpu.VMEM(latents.shape, BF16),
            pltpu.VMEM(latents.shape, BF16),
            pltpu.VMEM((G, w_qkv_tok.shape[1]), BF16),
            pltpu.VMEM((G, width), BF16),
            pltpu.VMEM((G, w_kv_read.shape[1]), BF16),
            pltpu.VMEM((groups, 2, 4 * nz, NLAT, lat_width), BF16),
            pltpu.VMEM((2, all_rows, here), BF16),
            pltpu.VMEM((lat_rows * lat_count * (here // HEAD), here), BF16),
            pltpu.VMEM((lat_count, lat_rows, here), BF16),
            pltpu.VMEM((lat_count, lat_rows, here), BF16),
            pltpu.VMEM((lat_rows * lat_count * (here // HEAD), 1), F32),
            pltpu.VMEM((lat_rows * lat_count * (here // HEAD), 1), F32),
            pltpu.VMEM((lat_rows * lat_count * (here // HEAD), here), F32),
            dma((8,)),
            dma((groups, nz)),
            dma((groups, nz)),
            dma((groups, PARTS)),
            dma((groups, PARTS)),
            dma((groups, 2 * PARTS)),
            dma((groups, 2 * PARTS)),
            dma((groups, 4 * PARTS)),
            dma((groups, 4 * PARTS)),
            dma((3,)),
            dma((3,)),
            dma((3,)),
            dma((3,)),
        ],
        compiler_params=pltpu.CompilerParams(
            collective_id=0, has_side_effects=True, vmem_limit_bytes=67043328
        ),
    )(
        tokens, latents, gain_self[None], w_qkv_tok, w_o_tok, gain_read[None], w_kv_read,
        gain_lat[None], w_q_read, gain_glob[None], w_qkv_glob, w_o_glob, gain_write[None],
        w_q_write, gain_wlat[None], w_kv_write,
    )
    per_group = pl.BlockSpec((G, width), lambda g: (g, 0))
    per_lat = pl.BlockSpec((NLAT, lat_width), lambda g: (g, 0))
    return pl.pallas_call(
        back,
        grid=(groups,),
        out_shape=(
            jax.ShapeDtypeStruct(tokens.shape, BF16),
            jax.ShapeDtypeStruct(latents.shape, BF16),
        ),
        in_specs=[
            per_group,
            per_lat,
            per_group,
            pl.BlockSpec((NLAT, key_vals.shape[1]), lambda g: (g, 0)),
        ],
        out_specs=(per_group, per_lat),
    )(query, final, mid, key_vals)


def solution(mesh):
    rows = P(("dp", "lat"), None)
    whole = P()
    placed = (
        rows, rows, whole, whole, whole, whole, whole, whole, whole, whole,
        P(None, None, "lat"), P("lat", None), whole, whole, whole, whole,
    )
    return jax.shard_map(
        local, mesh=mesh, in_specs=placed, out_specs=(rows, rows), check_vma=False
    )
```

profile of v0, /device:TPU:0, one launch (start us, length us, event | category | flops | bytes accessed | tf_op | source)
XLA Modules:
  0.0 56.7 jit_solution(8345326458441282973)
XLA Ops:
  0.6 51.9 %shard_map.167 = (bf16[768,512]{1,0:T(8,128)(2,1)}, bf16[48,1024]{1,0:T(8,128)(2,1)}, bf16[768,512]{1,0:T(8,128)(2,1)}, bf16[48,1024]{1,0:T(8,128)(2,1)}) custom-call(bf16[768,512]{1,0:T(8,128)(2,1)} %tok.1, bf16[48,1024]{1,0:T(8,128)(2,1)} %lat_in.1, f32[1,512]{1,0:T(1,128)} %bitcast.9, bf16[512,1536]{1,0:T(8,128)(2,1)} %w_qkv_h.1, bf16[512,512]{1,0:T(8,128)(2,1)} %w_o_h.1, ...), custom_call_target="tpu_custom_call" | custom-call | tf_op jit(solution)/shard_map/pallas_call | solution.py:477
  52.5 4.2 %shard_map.168 = (bf16[768,512]{1,0:T(8,128)(2,1)}, bf16[48,1024]{1,0:T(8,128)(2,1)}) custom-call(bf16[768,512]{1,0:T(8,128)(2,1)} %get-tuple-element.6.query, bf16[48,1024]{1,0:T(8,128)(2,1)} %get-tuple-element.7.final, bf16[768,512]{1,0:T(8,128)(2,1)} %get-tuple-element.8.mid, bf16[48,1024]{1,0:T(8,128)(2,1)} %get-tuple-element.9.key_vals), custom_call_target="tpu_custom_call" | custom-call | tf_op jit(solution)/shard_map/pallas_call | solution.py:533
where the time goes:
time: 56.9 us; the launch traced here: 56.7 us
  Pallas kernels  56 us (98%)
  between operations  0.64 us (1%)
    pallas_call x1, Pallas kernels, local(): pl.pallas_call(functools.partial(kernel, dp_count, lat_count), out_shape=...  51.9 us
    pallas_call x1, Pallas kernels, local(): pl.pallas_call(back, grid=(groups,), out_shape=(jax.ShapeDtypeStruct(toke...  4.15 us

commit v1 on v0

--- a/solution.py
+++ b/solution.py
@@ -158,7 +158,6 @@
     lax.fori_loop(1, nz, greet, 0)
     for peer in ((dp_x, lat), (dp, lat_y), (dp, partner), (dp, diag)):
         pl.semaphore_signal(barrier, inc=1, device_id=peer, device_id_type=MESH)
-    pl.semaphore_wait(barrier, nz + 3)
 
     def remote(src, dst, send_sem, recv_sem, peer):
         return pltpu.make_async_remote_copy(
@@ -166,13 +165,16 @@
             device_id_type=MESH,
         )
 
-    wo_first = [
-        remote(w_og_h, w_og.at[lat], wo_send.at[0], wo_recv.at[0], (dp, partner)),
-        remote(w_og_h, w_og.at[lat], wo_send.at[1], wo_recv.at[1], (dp, lat_y)),
-    ]
-    wo_relay = remote(w_og.at[lat_y], w_og.at[lat_y], wo_send.at[2], wo_recv.at[2], (dp, partner))
-    for copy in wo_first:
-        copy.start()
+    wo_share = remote(w_og_h, w_og.at[lat], wo_send.at[0], wo_recv.at[0], (dp, partner))
+    wo_cross, wo_relay = [], []
+    wo_rows = w_og_h.shape[0] // 2
+    for i in range(2):
+        part_rows = pl.ds(i * wo_rows, wo_rows)
+        there = w_og.at[lat_y, part_rows]
+        wo_cross.append(
+            remote(w_og_h.at[part_rows], w_og.at[lat, part_rows], wo_send.at[1 + i], wo_recv.at[1 + i], (dp, lat_y))
+        )
+        wo_relay.append(remote(there, there, wo_send.at[3 + i], wo_recv.at[3 + i], (dp, partner)))
 
     def piece(g, start, count):
         return gath.at[g, core, pl.ds(start, count)]
@@ -197,7 +199,14 @@
             piece(g, start, run), c_send.at[g, k], c_recv.at[g, k], (dp, partner)
         )
 
-    def z_copy(g, offset):
+    late_half = z * 2 // nz
+
+    def near(o):
+        q = z // run
+        return q + o - 2 * ((q % 2) * (o % 2) + 2 * (q // 2) * (o // 2))
+
+    def z_copy(g, step):
+        offset = late_half * step + (1 - late_half) * (nz - step)
         return remote(
             gath.at[g, core, me], gath.at[g, core, me], z_send.at[g, (z + offset) % nz],
             z_recv.at[g, z], ((z + offset) % nz * 2 + x, lat),
@@ -222,7 +231,7 @@
 
     def stage_one(g, low, high):
         def body(o):
-            p = (z // run + o) % PARTS
+            p = near(o)
             each(0, run, lambda i: z_arrived(g, p * run + i))
             on_first(g, p).start()
             on_second(g, 0, p).start()
@@ -230,17 +239,17 @@
 
         each(low, high, body)
 
-    def stage_two(g):
+    def stage_two(g, low=0, high=PARTS):
         def body(o):
-            p = (z // run + o) % PARTS
+            p = near(o)
             on_first(g, p).wait_recv()
             on_second(g, 1, p).start()
             share(g, 1, p).start()
 
-        each(0, PARTS, body)
+        each(low, high, body)
 
     def second_arrived(g, half, o):
-        p = (z // run + o) % PARTS
+        p = near(o)
         on_second(g, half, p).wait_recv()
         share(g, 2 + half, p).start()
 
@@ -293,15 +302,29 @@
         z_start(g)
         stage_one(g, 0, 1)
 
+    def scope(name):
+        return jax.named_scope(name)
+
     last = groups - 1
     for g in range(groups):
-        self_part(g)
+        with scope(f"self{g}"):
+            self_part(g)
+        if g == 0:
+            with scope("bar"):
+                pl.semaphore_wait(barrier, nz + 3)
+            wo_share.start()
+            wo_cross[0].start()
         if g >= 2:
-            stage_one(g - 2, 1, PARTS)
-            if g == 2:
-                wo_first[1].wait_recv()
-                wo_relay.start()
-        read_part(g)
+            with scope("fwdA"):
+                stage_one(g - 2, 2, PARTS)
+                if g == 2:
+                    wo_cross[0].wait_recv()
+                    wo_relay[0].start()
+        with scope(f"read{g}"):
+            read_part(g)
+        if g >= 1 and g < last:
+            with scope("fwdB"):
+                stage_one(g - 1, 1, 2)
 
     block_rows = 4 * nz * NLAT
     tile = min(block_rows, G)
@@ -317,41 +340,52 @@
 
         lax.fori_loop(0, block_rows // tile, one, 0)
 
+    with scope("fwdC"):
+        for g in range(last - 1):
+            stage_two(g)
+        stage_one(last - 1, 1, PARTS)
+    loads[5].wait()
+    with scope("wq"):
+        for g in range(groups):
+            rows = pl.ds(g * G, G)
+            query = dot(rms_norm(mid[rows, :], g_write[...]), w_qw[...]).astype(BF16)
+            tok_out[rows, :] = query * jnp.asarray(SCALE, BF16)
+    loads[4].wait()
+    with scope("fwdD"):
+        for g in range(last - 1):
+            stage_three(g)
+        stage_two(last - 1)
     for g in range(last - 1):
-        stage_two(g)
-    loads[5].wait()
-    for g in range(groups):
-        rows = pl.ds(g * G, G)
-        query = dot(rms_norm(mid[rows, :], g_write[...]), w_qw[...]).astype(BF16)
-        tok_out[rows, :] = query * jnp.asarray(SCALE, BF16)
-    stage_one(last - 1, 1, PARTS)
-    loads[4].wait()
-    for g in range(last - 1):
-        stage_three(g)
-    stage_two(last - 1)
-    for g in range(last - 1):
-        gathered(g)
-        project(g, 0)
-        project(g, 1)
-    stage_one(last, 1, PARTS)
-    stage_two(last)
-    stage_three(last - 1)
-    gathered(last - 1)
-    project(last - 1, 0)
-    project(last - 1, 1)
+        with scope("gath0"):
+            gathered(g)
+        with scope("proj0"):
+            project(g, 0)
+            project(g, 1)
+    with scope("fwdE"):
+        stage_one(last, 1, PARTS)
+        stage_three(last - 1)
+    with scope("fwdF"):
+        stage_two(last)
+        wo_cross[1].start()
+    with scope("gath1"):
+        gathered(last - 1)
+    with scope("proj1"):
+        project(last - 1, 0)
+        project(last - 1, 1)
     own_p = z // run
 
-    @pl.when(core == 1)
-    def _():
-        on_second(last, 0, own_p).wait_recv()
-        share(last, 2, own_p).start()
-        for line in range(2):
-            share(last, line, own_p).wait_recv()
-
-    @pl.when(core == 0)
-    def _():
-        for line in (0, 2):
-            share(last, line, own_p).wait_recv()
+    with scope('ownw'):
+        @pl.when(core == 1)
+        def _():
+            on_second(last, 0, own_p).wait_recv()
+            share(last, 2, own_p).start()
+            for line in range(2):
+                share(last, line, own_p).wait_recv()
+
+        @pl.when(core == 0)
+        def _():
+            for line in (0, 2):
+                share(last, line, own_p).wait_recv()
 
     own = []
     for l in range(lat_count):
@@ -387,28 +421,35 @@
         qq[rows, :] = (both * (1.0 / total)).astype(BF16)
         return carry
 
-    lax.fori_loop(0, qq.shape[0] // part, attend_early, 0)
-
-    @pl.when(core == 1)
-    def _():
-        each(1, PARTS, lambda o: second_arrived(last, 0, o))
-        each(0, PARTS, lambda o: second_arrived(last, 1, o))
-        for line in range(2):
-            each(1, PARTS, lambda o: share(last, line, (own_p + o) % PARTS).wait_recv())
-        for line in range(2, 4):
-            each(0, PARTS, lambda p: share(last, line, p).wait_recv())
-
-    @pl.when(core == 0)
-    def _():
-        stage_three(last)
-        for line in (0, 2):
-            each(1, PARTS, lambda o: share(last, line, (own_p + o) % PARTS).wait_recv())
-        for line in (1, 3):
-            each(0, PARTS, lambda p: share(last, line, p).wait_recv())
-
-    project(last, 0)
-    project(last, 1)
-    lax.fori_loop(0, qq.shape[0] // part, attend_late, 0)
+    with scope("attE"):
+        lax.fori_loop(0, qq.shape[0] // part, attend_early, 0)
+
+    with scope('lastw'):
+        @pl.when(core == 1)
+        def _():
+            each(1, PARTS, lambda o: second_arrived(last, 0, o))
+            each(0, PARTS, lambda o: second_arrived(last, 1, o))
+            for line in range(2):
+                each(1, PARTS, lambda o: share(last, line, near(o)).wait_recv())
+            for line in range(2, 4):
+                each(0, PARTS, lambda p: share(last, line, p).wait_recv())
+
+        @pl.when(core == 0)
+        def _():
+            stage_three(last)
+            for line in (0, 2):
+                each(1, PARTS, lambda o: share(last, line, near(o)).wait_recv())
+            for line in (1, 3):
+                each(0, PARTS, lambda p: share(last, line, p).wait_recv())
+
+    with scope("proj2"):
+        project(last, 0)
+        project(last, 1)
+    with scope("woB"):
+        wo_cross[1].wait_recv()
+        wo_relay[1].start()
+    with scope("attL"):
+        lax.fori_loop(0, qq.shape[0] // part, attend_late, 0)
     result = fold_heads(qq[...], heads)
     for l in range(lat_count):
         msend[l] = result[l * lat_rows : (l + 1) * lat_rows]
@@ -419,10 +460,12 @@
     mrecv[lat] = msend[lat]
     loads[7].wait()
     loads[6].wait()
-    wo_first[0].wait_recv()
-    wo_relay.wait_recv()
-    for copy in mix_copies:
-        copy.wait_recv()
+    with scope("mixw"):
+        wo_share.wait_recv()
+        for copy in wo_relay:
+            copy.wait_recv()
+        for copy in mix_copies:
+            copy.wait_recv()
     total = dot(mrecv[0], w_og[0])
     for l in range(1, lat_count):
         total = total + dot(mrecv[l], w_og[l])
@@ -430,7 +473,7 @@
     lat_out[...] = final
     lfin[...] = dot(rms_norm(final, g_wlat[...]), w_kvw[...]).astype(BF16)
 
-    for copy in wo_first + [wo_relay] + mix_copies:
+    for copy in [wo_share] + wo_cross + wo_relay + mix_copies:
         copy.wait_send()
     for g in range(groups):
         each(1, nz, lambda offset: z_copy(g, offset).wait_send())
@@ -515,8 +558,8 @@
             dma((groups, 2 * PARTS)),
             dma((groups, 4 * PARTS)),
             dma((groups, 4 * PARTS)),
-            dma((3,)),
-            dma((3,)),
+            dma((5,)),
+            dma((5,)),
             dma((3,)),
             dma((3,)),
         ],

time: 56.9 us -> 49.6 us (0.87)
  Pallas kernels: 56 us -> 48.8 us
    pallas_call x1, Pallas kernels: 51.9 us -> 44.6 us  [local(): pl.pallas_call(functools.partial(kernel, dp_count, lat_count), out_shape=...]
where the time goes in v1:
time: 49.6 us; the launch traced here: 49.4 us
  Pallas kernels  48.8 us (98%)
  between operations  0.64 us (1%)
    pallas_call x1, Pallas kernels, local(): pl.pallas_call(functools.partial(kernel, dp_count, lat_count), out_shape=...  44.6 us
    pallas_call x1, Pallas kernels, local(): pl.pallas_call(back, grid=(groups,), out_shape=(jax.ShapeDtypeStruct(toke...  4.15 us

profile of v1, /device:TPU:0, one launch (start us, length us, event | category | flops | bytes accessed | tf_op | source)
XLA Modules:
  0.0 49.4 jit_solution(11640503925691110184)
XLA Ops:
  0.6 44.6 %shard_map.167 = (bf16[768,512]{1,0:T(8,128)(2,1)}, bf16[48,1024]{1,0:T(8,128)(2,1)}, bf16[768,512]{1,0:T(8,128)(2,1)}, bf16[48,1024]{1,0:T(8,128)(2,1)}) custom-call(bf16[768,512]{1,0:T(8,128)(2,1)} %tok.1, bf16[48,1024]{1,0:T(8,128)(2,1)} %lat_in.1, f32[1,512]{1,0:T(1,128)} %bitcast.9, bf16[512,1536]{1,0:T(8,128)(2,1)} %w_qkv_h.1, bf16[512,512]{1,0:T(8,128)(2,1)} %w_o_h.1, ...), custom_call_target="tpu_custom_call" | custom-call | tf_op jit(solution)/shard_map/pallas_call | solution.py:520
  45.3 4.2 %shard_map.168 = (bf16[768,512]{1,0:T(8,128)(2,1)}, bf16[48,1024]{1,0:T(8,128)(2,1)}) custom-call(bf16[768,512]{1,0:T(8,128)(2,1)} %get-tuple-element.6.query, bf16[48,1024]{1,0:T(8,128)(2,1)} %get-tuple-element.7.final, bf16[768,512]{1,0:T(8,128)(2,1)} %get-tuple-element.8.mid, bf16[48,1024]{1,0:T(8,128)(2,1)} %get-tuple-element.9.key_vals), custom_call_target="tpu_custom_call" | custom-call | tf_op jit(solution)/shard_map/pallas_call | solution.py:576

commit v2 on v1

--- a/solution.py
+++ b/solution.py
@@ -11,6 +11,7 @@
 G = 256
 NLAT = 16
 SCALE = HEAD ** (-0.5)
+LOG2E = 1.4426950408889634
 MESH = pl.DeviceIdType.MESH
 PARTS = 4
 F32 = jnp.float32
@@ -53,7 +54,7 @@
 def softmax_mix(stacked, keys, values):
     scores = dot_nt(stacked, keys)
     peak = jnp.max(scores, axis=-1, keepdims=True)
-    weights = jnp.exp(scores - peak)
+    weights = jnp.exp2(scores - peak)
     total = jnp.sum(weights, axis=-1, keepdims=True)
     return dot(weights.astype(BF16), values) * (1.0 / total)
 
@@ -61,26 +62,34 @@
 def kernel(
     dp_count,
     lat_count,
-    tok,
-    lat_in,
-    g_self,
+    tok_h,
+    lat_h,
+    g_self_h,
     w_qkv_h,
     w_o_h,
-    g_read,
+    g_read_h,
     w_kvr_h,
-    g_lat,
+    g_lat_h,
     w_qr_h,
-    g_glob,
+    g_glob_h,
     w_glob_h,
     w_og_h,
-    g_write,
+    g_write_h,
     w_qw_h,
-    g_wlat,
+    g_wlat_h,
     w_kvw_h,
     tok_out,
     lat_out,
     mid,
     lfin,
+    tok,
+    lat_in,
+    g_self,
+    g_read,
+    g_lat,
+    g_glob,
+    g_write,
+    g_wlat,
     w_qkv,
     w_o,
     w_kvr,
@@ -90,10 +99,9 @@
     w_qw,
     w_kvw,
     lmid,
-    rq,
     packed,
     mixed,
-    kvr,
+    read_q,
     gath,
     kv,
     qq,
@@ -116,10 +124,10 @@
     m_send,
     m_recv,
 ):
-    width = tok.shape[1]
-    lat_width = lat_in.shape[1]
-    groups = tok.shape[0] // G
-    lat_rows = lat_in.shape[0]
+    width = tok_h.shape[1]
+    lat_width = lat_h.shape[1]
+    groups = tok_h.shape[0] // G
+    lat_rows = lat_h.shape[0]
     nz = dp_count // 2
     dp = lax.axis_index("dp")
     lat = lax.axis_index("lat")
@@ -140,12 +148,19 @@
     run = nz // PARTS
 
     loads = []
-    for i, (src, dst) in enumerate(
-        ((w_qkv_h, w_qkv), (w_o_h, w_o), (w_qr_h, w_qr), (w_kvr_h, w_kvr), (w_glob_h, w_glob),
-         (w_qw_h, w_qw), (w_kvw_h, w_kvw), (w_og_h, w_og.at[lat]))
-    ):
-        loads.append(pltpu.make_async_copy(src, dst, load_sem.at[i]))
+
+    def load(src, dst):
+        loads.append(pltpu.make_async_copy(src, dst, load_sem.at[len(loads)]))
         loads[-1].start()
+        return loads[-1]
+
+    def group_load(g):
+        rows = pl.ds(g * G, G)
+        return load(tok_h.at[rows], tok.at[rows])
+
+    tok_load = [group_load(0)]
+    gain_load = [load(g_self_h, g_self)]
+    qkv_load = load(w_qkv_h, w_qkv)
 
     barrier = pltpu.get_barrier_semaphore()
 
@@ -158,6 +173,14 @@
     lax.fori_loop(1, nz, greet, 0)
     for peer in ((dp_x, lat), (dp, lat_y), (dp, partner), (dp, diag)):
         pl.semaphore_signal(barrier, inc=1, device_id=peer, device_id_type=MESH)
+
+    o_load = load(w_o_h, w_o)
+    for src, dst in ((lat_h, lat_in), (g_lat_h, g_lat), (g_read_h, g_read), (g_glob_h, g_glob), (g_write_h, g_write), (g_wlat_h, g_wlat)):
+        gain_load.append(load(src, dst))
+    qr_load = load(w_qr_h, w_qr)
+    kvr_load = load(w_kvr_h, w_kvr)
+    for g in range(1, groups):
+        tok_load.append(group_load(g))
 
     def remote(src, dst, send_sem, recv_sem, peer):
         return pltpu.make_async_remote_copy(
@@ -261,40 +284,63 @@
         for line in range(4):
             each(0, PARTS, lambda p: share(g, line, p).wait_recv())
 
+    later = []
+
     def self_part(g):
         rows = pl.ds(g * G, G)
+        tok_load[g].wait()
+        if g == 0:
+            gain_load[0].wait()
         group = tok[rows, :]
         normed = rms_norm(group, g_self[...])
         if g == 0:
-            loads[0].wait()
-        packed[...] = dot(normed, w_qkv[...]).astype(BF16)
+            qkv_load.wait()
+            for src, dst in ((w_glob_h, w_glob), (w_qw_h, w_qw), (w_kvw_h, w_kvw), (w_og_h, w_og.at[lat])):
+                later.append(load(src, dst))
+        packed[:, :width] = (dot(normed, w_qkv[:, :width]) * (SCALE * LOG2E)).astype(BF16)
+        packed[:, width:] = dot(normed, w_qkv[:, width:]).astype(BF16)
         for pair in range(width // (2 * HEAD)):
             at = pair * 2 * HEAD
-            query = packed[:, at : at + 2 * HEAD] * jnp.asarray(SCALE, BF16)
+            query = packed[:, at : at + 2 * HEAD]
             keys = packed[:, width + at : width + at + 2 * HEAD]
             values = packed[:, 2 * width + at : 2 * width + at + 2 * HEAD]
             out = softmax_mix(spread_heads(query, 2), keys, values)
             mixed[:, at : at + 2 * HEAD] = fold_heads(out, 2).astype(BF16)
         if g == 0:
-            loads[1].wait()
+            o_load.wait()
         mid[rows, :] = (group.astype(F32) + dot(mixed[...], w_o[...])).astype(BF16)
+
+    quad = 4 * HEAD
+
+    def read_queries():
+        for copy in gain_load[1:]:
+            copy.wait()
+        qr_load.wait()
+        query = dot(rms_norm(lat_in[...], g_lat[...]), w_qr[...])
+        query = (query * (SCALE * LOG2E)).astype(BF16)
+        kvr_load.wait()
+        for at in range(0, lat_width, quad):
+            keyed = dot_nt(spread_heads(query[:, at : at + quad], 4), w_kvr[:, at : at + quad]).astype(BF16)
+            for h in range(4):
+                for g in range(groups):
+                    start = h * lat_rows + g * NLAT
+                    head = at // HEAD + h
+                    read_q[g, head * NLAT : (head + 1) * NLAT, :] = keyed[start : start + NLAT, :]
 
     def read_part(g):
         if g == 0:
-            loads[2].wait()
-            query = dot(rms_norm(lat_in[...], g_lat[...]), w_qr[...]).astype(BF16)
-            rq[...] = query * jnp.asarray(SCALE, BF16)
-            loads[3].wait()
+            read_queries()
         rows = pl.ds(g * G, G)
         lrows = pl.ds(g * NLAT, NLAT)
-        kvr[...] = dot(rms_norm(mid[rows, :], g_read[...]), w_kvr[...]).astype(BF16)
-        quad = 4 * HEAD
+        normed = rms_norm(mid[rows, :], g_read[...])
+        scores = dot_nt(read_q[g], normed)
+        peak = jnp.max(scores, axis=-1, keepdims=True)
+        weights = jnp.exp2(scores - peak)
+        inverse = 1.0 / jnp.sum(weights, axis=-1, keepdims=True)
+        seen = (dot(weights.astype(BF16), normed) * inverse).astype(BF16)
         for at in range(0, lat_width, quad):
-            out = softmax_mix(
-                spread_heads(rq[lrows, at : at + quad], 4),
-                kvr[:, at : at + quad],
-                kvr[:, lat_width + at : lat_width + at + quad],
-            )
+            start = at // HEAD * NLAT
+            out = dot(seen[start : start + 4 * NLAT], w_kvr[:, lat_width + at : lat_width + at + quad])
             lmid[lrows, at : at + quad] = (
                 lat_in[lrows, at : at + quad].astype(F32) + fold_heads(out, 4)
             ).astype(BF16)
@@ -344,13 +390,13 @@
         for g in range(last - 1):
             stage_two(g)
         stage_one(last - 1, 1, PARTS)
-    loads[5].wait()
+    later[1].wait()
     with scope("wq"):
         for g in range(groups):
             rows = pl.ds(g * G, G)
             query = dot(rms_norm(mid[rows, :], g_write[...]), w_qw[...]).astype(BF16)
             tok_out[rows, :] = query * jnp.asarray(SCALE, BF16)
-    loads[4].wait()
+    later[0].wait()
     with scope("fwdD"):
         for g in range(last - 1):
             stage_three(g)
@@ -393,36 +439,41 @@
         index = ((x * 2 + ly) if lc == 0 else (ly * 2 + x)) * nz + z
         for g in range(groups):
             own.append(gath[g, lc, index])
-    query = dot(jnp.concatenate(own, axis=0), w_glob[0]).astype(BF16) * jnp.asarray(SCALE, BF16)
+    query = dot(jnp.concatenate(own, axis=0), w_glob[0])
+    query = (query * (SCALE * LOG2E)).astype(BF16)
     heads = query.shape[1] // HEAD
-    qq[...] = spread_heads(query, heads)
+    part = lat_rows * heads
+    for l in range(lat_count):
+        qq[l * part : (l + 1) * part, :] = spread_heads(query[l * lat_rows : (l + 1) * lat_rows], heads)
     early = last * 2 * block_rows
-    full = lat_rows * lat_count
-    part = full if early * full <= 2**20 else lat_rows
-
-    def attend_early(i, carry):
-        rows = pl.ds(pl.multiple_of(i * part, part), part)
+    wide = early * part <= 2**20
+    step = part if wide else part // heads
+
+    def attend_early(at):
+        rows = pl.ds(pl.multiple_of(at, 16), step)
         scores = dot_nt(qq[rows, :], kv[0, :early, :])
         peak = jnp.max(scores, axis=-1, keepdims=True)
-        weights = jnp.exp(scores - peak)
+        weights = jnp.exp2(scores - peak)
         top[rows, :] = peak
         norm[rows, :] = jnp.sum(weights, axis=-1, keepdims=True)
         acc[rows, :] = dot(weights.astype(BF16), kv[1, :early, :])
-        return carry
-
-    def attend_late(i, carry):
-        rows = pl.ds(pl.multiple_of(i * part, part), part)
+
+    def attend_late(at):
+        rows = pl.ds(pl.multiple_of(at, 16), step)
         scores = dot_nt(qq[rows, :], kv[0, early:, :])
         peak = jnp.maximum(top[rows, :], jnp.max(scores, axis=-1, keepdims=True))
-        weights = jnp.exp(scores - peak)
-        keep = jnp.exp(top[rows, :] - peak)
+        weights = jnp.exp2(scores - peak)
+        keep = jnp.exp2(top[rows, :] - peak)
         total = norm[rows, :] * keep + jnp.sum(weights, axis=-1, keepdims=True)
         both = acc[rows, :] * keep + dot(weights.astype(BF16), kv[1, early:, :])
-        qq[rows, :] = (both * (1.0 / total)).astype(BF16)
-        return carry
+        return both * (1.0 / total)
 
     with scope("attE"):
-        lax.fori_loop(0, qq.shape[0] // part, attend_early, 0)
+        if wide:
+            for l in range(lat_count):
+                attend_early(l * part)
+        else:
+            each(0, qq.shape[0] // step, lambda i: attend_early(i * step))
 
     with scope('lastw'):
         @pl.when(core == 1)
@@ -448,18 +499,29 @@
     with scope("woB"):
         wo_cross[1].wait_recv()
         wo_relay[1].start()
+    mix_copies = []
     with scope("attL"):
-        lax.fori_loop(0, qq.shape[0] // part, attend_late, 0)
-    result = fold_heads(qq[...], heads)
-    for l in range(lat_count):
-        msend[l] = result[l * lat_rows : (l + 1) * lat_rows]
-    mix_copies = []
-    for i, peer in enumerate((partner, lat_y, diag)):
-        mix_copies.append(remote(msend.at[peer], mrecv.at[lat], m_send.at[i], m_recv.at[i], (dp, peer)))
-        mix_copies[-1].start()
-    mrecv[lat] = msend[lat]
-    loads[7].wait()
-    loads[6].wait()
+        for i, peer in enumerate((diag, lat_y, partner, lat)):
+            if wide:
+                result = fold_heads(attend_late(peer * part), heads)
+            else:
+                def late_step(k, carry):
+                    at = peer * part + k * step
+                    qq[pl.ds(pl.multiple_of(at, 16), step), :] = attend_late(at).astype(BF16)
+                    return carry
+
+                lax.fori_loop(0, heads, late_step, 0)
+                result = fold_heads(qq[pl.ds(pl.multiple_of(peer * part, 16), part), :], heads)
+            if i < 3:
+                msend[peer] = result.astype(BF16)
+                mix_copies.append(
+                    remote(msend.at[peer], mrecv.at[lat], m_send.at[i], m_recv.at[i], (dp, peer))
+                )
+                mix_copies[-1].start()
+            else:
+                mrecv[lat] = result.astype(BF16)
+    later[3].wait()
+    later[2].wait()
     with scope("mixw"):
         wo_share.wait_recv()
         for copy in wo_relay:
@@ -525,9 +587,17 @@
             jax.ShapeDtypeStruct(tokens.shape, BF16),
             jax.ShapeDtypeStruct((lat_rows, w_kv_write.shape[1]), BF16),
         ),
-        in_specs=[vmem, vmem, vmem, hbm, hbm, vmem, hbm, vmem, hbm, vmem, hbm, hbm, vmem, hbm, vmem, hbm],
+        in_specs=[hbm] * 16,
         out_specs=(vmem,) * 4,
         scratch_shapes=[
+            pltpu.VMEM(tokens.shape, BF16),
+            pltpu.VMEM(latents.shape, BF16),
+            pltpu.VMEM((1, width), F32),
+            pltpu.VMEM((1, width), F32),
+            pltpu.VMEM((1, lat_width), F32),
+            pltpu.VMEM((1, lat_width), F32),
+            pltpu.VMEM((1, width), F32),
+            pltpu.VMEM((1, lat_width), F32),
             pltpu.VMEM(w_qkv_tok.shape, BF16),
             pltpu.VMEM(w_o_tok.shape, BF16),
             pltpu.VMEM(w_kv_read.shape, BF16),
@@ -537,10 +607,9 @@
             pltpu.VMEM(w_q_write.shape, BF16),
             pltpu.VMEM(w_kv_write.shape, BF16),
             pltpu.VMEM(latents.shape, BF16),
-            pltpu.VMEM(latents.shape, BF16),
             pltpu.VMEM((G, w_qkv_tok.shape[1]), BF16),
             pltpu.VMEM((G, width), BF16),
-            pltpu.VMEM((G, w_kv_read.shape[1]), BF16),
+            pltpu.VMEM((groups, lat_width // HEAD * NLAT, width), BF16),
             pltpu.VMEM((groups, 2, 4 * nz, NLAT, lat_width), BF16),
             pltpu.VMEM((2, all_rows, here), BF16),
             pltpu.VMEM((lat_rows * lat_count * (here // HEAD), here), BF16),
@@ -549,7 +618,7 @@
             pltpu.VMEM((lat_rows * lat_count * (here // HEAD), 1), F32),
             pltpu.VMEM((lat_rows * lat_count * (here // HEAD), 1), F32),
             pltpu.VMEM((lat_rows * lat_count * (here // HEAD), here), F32),
-            dma((8,)),
+            dma((15 + groups,)),
             dma((groups, nz)),
             dma((groups, nz)),
             dma((groups, PARTS)),

time: 49.6 us -> 47.7 us (0.962)
  Pallas kernels: 48.8 us -> 46.9 us
    pallas_call x1, Pallas kernels: 44.6 us -> 42.7 us  [local(): pl.pallas_call(functools.partial(kernel, dp_count, lat_count), out_shape=...]
where the time goes in v2:
time: 47.7 us; the launch traced here: 47.5 us
  Pallas kernels  46.9 us (98%)
  between operations  0.65 us (1%)
    pallas_call x1, Pallas kernels, local(): pl.pallas_call(functools.partial(kernel, dp_count, lat_count), out_shape=...  42.7 us
    pallas_call x1, Pallas kernels, local(): pl.pallas_call(back, grid=(groups,), out_shape=(jax.ShapeDtypeStruct(toke...  4.15 us

profile of v2, /device:TPU:0, one launch (start us, length us, event | category | flops | bytes accessed | tf_op | source)
XLA Modules:
  0.0 47.5 jit_solution(7969041401829297927)
XLA Ops:
  0.6 42.7 %shard_map.167 = (bf16[768,512]{1,0:T(8,128)(2,1)}, bf16[48,1024]{1,0:T(8,128)(2,1)}, bf16[768,512]{1,0:T(8,128)(2,1)}, bf16[48,1024]{1,0:T(8,128)(2,1)}) custom-call(bf16[768,512]{1,0:T(8,128)(2,1)} %tok_h.1, bf16[48,1024]{1,0:T(8,128)(2,1)} %lat_h.1, f32[1,512]{1,0:T(1,128)} %bitcast.9, bf16[512,1536]{1,0:T(8,128)(2,1)} %w_qkv_h.1, ...), custom_call_target="tpu_custom_call" | custom-call | tf_op jit(solution)/shard_map/pallas_call | solution.py:582
  43.4 4.2 %shard_map.168 = (bf16[768,512]{1,0:T(8,128)(2,1)}, bf16[48,1024]{1,0:T(8,128)(2,1)}) custom-call(bf16[768,512]{1,0:T(8,128)(2,1)} %get-tuple-element.6.query, bf16[48,1024]{1,0:T(8,128)(2,1)} %get-tuple-element.7.final, bf16[768,512]{1,0:T(8,128)(2,1)} %get-tuple-element.8.mid, bf16[48,1024]{1,0:T(8,128)(2,1)} %get-tuple-element.9.key_vals), custom_call_target="tpu_custom_call" | custom-call | tf_op jit(solution)/shard_map/pallas_call | solution.py:645

commit v3 on v2

v3 whole, which is shorter than its diff:
```python
import functools

import jax
import jax.numpy as jnp
from jax import lax
from jax.experimental import pallas as pl
from jax.experimental.pallas import tpu as pltpu
from jax.sharding import PartitionSpec as P

HEAD = 64
G = 256
NLAT = 16
SCALE = HEAD ** (-0.5)
LOG2E = 1.4426950408889634
MESH = pl.DeviceIdType.MESH
F32 = jnp.float32
BF16 = jnp.bfloat16


def rms_norm(values, gain):
    floats = values.astype(F32)
    factor = lax.rsqrt(jnp.mean(floats * floats, axis=-1, keepdims=True) + 1e-06)
    return (floats * factor * gain).astype(BF16)


def dot(a, b):
    return jnp.dot(a, b, preferred_element_type=F32)


def dot_nt(a, b):
    return lax.dot_general(a, b, (((1,), (1,)), ((), ())), preferred_element_type=F32)


def dot_tn(a, b):
    return lax.dot_general(a, b, (((0,), (0,)), ((), ())), preferred_element_type=F32)


def spread_heads(query, count):
    lane_head = lax.broadcasted_iota(jnp.int32, query.shape, 1) // HEAD
    zero = jnp.zeros_like(query)
    return jnp.concatenate([jnp.where(lane_head == h, query, zero) for h in range(count)], axis=0)


def fold_heads(stacked, count):
    rows = stacked.shape[0] // count
    lane_head = lax.broadcasted_iota(jnp.int32, (rows, stacked.shape[1]), 1) // HEAD
    out = stacked[:rows]
    for h in range(1, count):
        out = jnp.where(lane_head == h, stacked[h * rows : (h + 1) * rows], out)
    return out


def softmax_mix(stacked, keys, values):
    scores = dot_nt(stacked, keys)
    peak = jnp.max(scores, axis=-1, keepdims=True)
    weights = jnp.exp2(scores - peak)
    total = jnp.sum(weights, axis=-1, keepdims=True)
    return dot(weights.astype(BF16), values) * (1.0 / total)


def kernel(
    dp_count, lat_count,
    tok_h, lat_h, g_self_h, w_qkv_h, w_o_h, g_read_h, w_kvr_h, g_lat_h, w_qr_h, g_glob_h,
    w_glob_h, w_og_h, g_write_h, w_qw_h, g_wlat_h, w_kvw_h,
    tok_out, lat_out, mid, lfin,
    tok, lat_in, g_self, g_read, g_lat, g_glob, g_write, g_wlat,
    w_qkv, w_o, w_kvr, w_qr, w_glob, w_og, w_qw, w_kvw,
    lmid, packed, mixed, read_q, normed_lat, outgoing, arrived, results, returned, mix,
    load_sem, l_send, l_recv, s_send, s_recv, t_send, t_recv, wo_send, wo_recv,
):
    width = tok_h.shape[1]
    lat_width = lat_h.shape[1]
    groups = tok_h.shape[0] // G
    lat_rows = lat_h.shape[0]
    last = groups - 1
    here = w_glob_h.shape[2] // HEAD
    slots = dp_count // here
    line = lat_count * NLAT
    lanes = 2 * HEAD
    dp = lax.axis_index("dp")
    lat = lax.axis_index("lat")
    head, slot = dp // slots, dp % slots
    core = lat % 2
    lat_y = (lat + 2) % 4
    partner = lat + 1 - 2 * core
    diag = (partner + 2) % 4
    upper = head * 2 // here

    def scope(name):
        return jax.named_scope(name)

    def each(low, high, body):
        def one(i, carry):
            body(i)
            return carry

        lax.fori_loop(low, high, one, 0)

    loads = []

    def load(src, dst):
        loads.append(pltpu.make_async_copy(src, dst, load_sem.at[len(loads)]))
        loads[-1].start()
        return loads[-1]

    def group_load(g):
        rows = pl.ds(g * G, G)
        return load(tok_h.at[rows], tok.at[rows])

    tok_load = [group_load(0)]
    gain_load = [load(g_self_h, g_self)]
    qkv_load = []
    for i in range(3):
        columns = pl.ds(i * width, width)
        qkv_load.append(load(w_qkv_h.at[:, columns], w_qkv.at[:, columns]))

    barrier = pltpu.get_barrier_semaphore()

    def greet(peer):
        pl.semaphore_signal(barrier, inc=1, device_id=peer, device_id_type=MESH)

    each(1, dp_count, lambda o: greet(((dp + o) % dp_count, lat)))
    for o in range(1, lat_count):
        each(0, here, lambda h: greet((h * slots + slot, (lat + o) % lat_count)))

    o_load = load(w_o_h, w_o)
    for src, dst in (
        (lat_h, lat_in), (g_lat_h, g_lat), (g_read_h, g_read), (g_glob_h, g_glob), (g_write_h, g_write),
        (g_wlat_h, g_wlat),
    ):
        gain_load.append(load(src, dst))
    qr_load = load(w_qr_h, w_qr)
    kvr_load = load(w_kvr_h, w_kvr)
    for g in range(1, groups):
        tok_load.append(group_load(g))
    later = []

    def remote(src, dst, send_sem, recv_sem, peer):
        return pltpu.make_async_remote_copy(
            src_ref=src, dst_ref=dst, send_sem=send_sem, recv_sem=recv_sem, device_id=peer,
            device_id_type=MESH,
        )

    def landed(ref, sem):
        pltpu.make_async_copy(ref, ref, sem).wait()

    wo_share = remote(w_og_h, w_og.at[lat], wo_send.at[0], wo_recv.at[0], (dp, partner))
    wo_cross, wo_relay = [], []
    wo_rows = w_og_h.shape[0] // 2
    for i in range(2):
        part_rows = pl.ds(i * wo_rows, wo_rows)
        there = w_og.at[lat_y, part_rows]
        wo_cross.append(
            remote(w_og_h.at[part_rows], w_og.at[lat, part_rows], wo_send.at[1 + i], wo_recv.at[1 + i], (dp, lat_y))
        )
        wo_relay.append(remote(there, there, wo_send.at[3 + i], wo_recv.at[3 + i], (dp, partner)))

    def lat_copy(g, i):
        own = normed_lat.at[g, lat]
        peer = (diag, lat_y, partner)[i]
        return remote(own, own, l_send.at[g, i], l_recv.at[g, lat], (dp, peer))

    def far(i):
        return upper * i + (1 - upper) * (here - 1 - i)

    def to_head(g, h, j):
        rows = pl.ds(0, line)
        src, dst = outgoing.at[g, h], arrived.at[g, dp]
        if j is not None:
            src, dst = src.at[rows], dst.at[rows]
        spot = 0 if j is None else j
        peer = (h * slots + (slot + spot) % slots, lat)
        return remote(src, dst, s_send.at[g, h * slots + spot], s_recv.at[g, dp], peer)

    def spread(g):
        def one(i):
            h = far(i)

            @pl.when(h != head)
            def _():
                to_head(g, h, None).start()

            each(1, slots, lambda j: to_head(g, h, j).start())

        each(0, here, one)
        arrived[g, dp] = outgoing[g, head]

    def gathered(g):
        def one(h):
            @pl.when(h != head)
            def _():
                source = h * slots + slot
                landed(arrived.at[g, source], s_recv.at[g, source])

            def other(j):
                source = h * slots + (slot + j) % slots
                landed(arrived.at[g, source, pl.ds(0, line)], s_recv.at[g, source])

            each(1, slots, other)

        each(0, here, one)

    def low_lanes(rows):
        return lax.broadcasted_iota(jnp.int32, (rows, lanes), 1) < HEAD

    def swap(values):
        return pltpu.roll(values, HEAD, 1)

    def project(g):
        for i in range(1, lat_count):
            source = (lat + i) % lat_count
            landed(normed_lat.at[g, source], l_recv.at[g, source])
        rows = normed_lat[g].reshape(line, lat_width)
        queries = dot(rows, w_glob[0]) * (SCALE * LOG2E)
        keys = dot(rows, w_glob[1])
        values = dot(rows, w_glob[2])
        low, half = low_lanes(line), line // 2
        for h in range(0, here, 2):
            at = slice(h * HEAD, h * HEAD + lanes)
            k, v, q = keys[:, at], values[:, at], queries[:, at]
            outgoing[g, h, :line] = jnp.where(low, k, swap(v)).astype(BF16)
            outgoing[g, h + 1, :line] = jnp.where(low, swap(k), v).astype(BF16)
            q_swap = swap(q)
            outgoing[g, h, line:] = jnp.where(low[:half], q[:half], q_swap[half:]).astype(BF16)
            outgoing[g, h + 1, line:] = jnp.where(low[:half], q_swap[:half], q[half:]).astype(BF16)
        spread(g)

    def self_part(g):
        rows = pl.ds(g * G, G)
        tok_load[g].wait()
        if g == 0:
            gain_load[0].wait()
        group = tok[rows, :]
        normed = rms_norm(group, g_self[...])
        if g == 0:
            qkv_load[0].wait()
        packed[:, :width] = (dot(normed, w_qkv[:, :width]) * (SCALE * LOG2E)).astype(BF16)
        if g == 0:
            qkv_load[1].wait()
            qkv_load[2].wait()
            for src, dst in (
                (w_glob_h, w_glob), (w_qw_h, w_qw), (w_kvw_h, w_kvw), (w_og_h, w_og.at[lat]),
            ):
                later.append(load(src, dst))
        packed[:, width:] = dot(normed, w_qkv[:, width:]).astype(BF16)
        for pair in range(width // lanes):
            at = pair * lanes
            query = packed[:, at : at + lanes]
            keys = packed[:, width + at : width + at + lanes]
            values = packed[:, 2 * width + at : 2 * width + at + lanes]
            out = softmax_mix(spread_heads(query, 2), keys, values)
            mixed[:, at : at + lanes] = fold_heads(out, 2).astype(BF16)
        if g == 0:
            o_load.wait()
        mid[rows, :] = (group.astype(F32) + dot(mixed[...], w_o[...])).astype(BF16)

    quad = 4 * HEAD

    def read_queries():
        for copy in gain_load[1:]:
            copy.wait()
        qr_load.wait()
        query = dot(rms_norm(lat_in[...], g_lat[...]), w_qr[...])
        query = (query * (SCALE * LOG2E)).astype(BF16)
        kvr_load.wait()
        for at in range(0, lat_width, quad):
            keyed = dot_nt(spread_heads(query[:, at : at + quad], 4), w_kvr[:, at : at + quad]).astype(BF16)
            for h in range(4):
                for g in range(groups):
                    start = h * lat_rows + g * NLAT
                    at_head = at // HEAD + h
                    read_q[g, at_head * NLAT : (at_head + 1) * NLAT, :] = keyed[start : start + NLAT, :]

    def read_part(g):
        if g == 0:
            read_queries()
        rows = pl.ds(g * G, G)
        lrows = pl.ds(g * NLAT, NLAT)
        normed = rms_norm(mid[rows, :], g_read[...])
        scores = dot_nt(read_q[g], normed)
        peak = jnp.max(scores, axis=-1, keepdims=True)
        weights = jnp.exp2(scores - peak)
        inverse = 1.0 / jnp.sum(weights, axis=-1, keepdims=True)
        seen = (dot(weights.astype(BF16), normed) * inverse).astype(BF16)
        for at in range(0, lat_width, quad):
            start = at // HEAD * NLAT
            out = dot(seen[start : start + 4 * NLAT], w_kvr[:, lat_width + at : lat_width + at + quad])
            lmid[lrows, at : at + quad] = (
                lat_in[lrows, at : at + quad].astype(F32) + fold_heads(out, 4)
            ).astype(BF16)
        normed_lat[g, lat] = rms_norm(lmid[lrows, :], g_glob[...])
        for i in range(3):
            lat_copy(g, i).start()

    for g in range(groups):
        with scope(f"self{g}"):
            self_part(g)
        if g == 0:
            with scope("bar"):
                pl.semaphore_wait(barrier, dp_count - 1 + here * (lat_count - 1))
            wo_share.start()
        with scope(f"read{g}"):
            read_part(g)
        if g == 1:
            later[0].wait()
        if 1 <= g < last:
            with scope(f"proj{g - 1}"):
                project(g - 1)
    for copy in wo_cross:
        copy.start()
    with scope("projM"):
        project(last - 1)
    later[1].wait()
    with scope("wq"):
        for g in range(groups):
            rows = pl.ds(g * G, G)
            query = dot(rms_norm(mid[rows, :], g_write[...]), w_qw[...]).astype(BF16)
            tok_out[rows, :] = query * jnp.asarray(SCALE, BF16)
    with scope("projL"):
        project(last)
    later[2].wait()
    later[3].wait()
    for g in range(last):
        with scope(f"gath{g}"):
            gathered(g)
    with scope("wo0"):
        wo_cross[0].wait_recv()
        wo_relay[0].start()
    with scope("gathL"):
        gathered(last)

    def queries_of(c):
        parts = []
        for g in range(groups):
            pack = arrived[g, c * slots + slot, line:].astype(F32)
            low = low_lanes(line // 2)
            parts.append(jnp.where(low, pack, 0.0))
            parts.append(jnp.where(low, swap(pack), 0.0))
        return jnp.concatenate(parts, axis=0).astype(BF16)

    def attend(c):
        query = queries_of(c)
        if dp_count * line * groups <= 2048:
            key_vals = jnp.concatenate(
                [arrived[g, d, :line] for g in range(groups) for d in range(dp_count)], axis=0
            )
            return softmax_mix(query, key_vals, key_vals)

        def fold(i, carry):
            peak, total, acc = carry
            for g in range(groups):
                key_vals = arrived[g, i, :line]
                scores = dot_nt(query, key_vals)
                new = jnp.maximum(peak, jnp.max(scores, axis=-1, keepdims=True))
                weights = jnp.exp2(scores - new)
                keep = jnp.exp2(peak - new)
                total = total * keep + jnp.sum(weights, axis=-1, keepdims=True)
                acc = acc * keep + dot(weights.astype(BF16), key_vals)
                peak = new
            return peak, total, acc

        rows = query.shape[0]
        first = (
            jnp.full((rows, 1), -jnp.inf, F32), jnp.zeros((rows, 1), F32), jnp.zeros((rows, lanes), F32)
        )
        _, total, acc = lax.fori_loop(0, dp_count, fold, first)
        return acc * (1.0 / total)

    mine = lat * here + head

    def result_copy(c, i):
        to = (lat + i) % lat_count
        return remote(
            results.at[c, to], returned.at[mine], t_send.at[c, to], t_recv.at[mine], (c * slots + slot, to)
        )

    with scope("att"):
        for i in range(here):
            c = (head + 1 + i) % here
            out = attend(c)
            low = low_lanes(line)
            for k in range(0, groups, 2):
                even = out[k * line : (k + 1) * line]
                odd = out[(k + 1) * line : (k + 2) * line] if k + 1 < groups else even
                pair = jnp.where(low, swap(even), odd).astype(BF16)
                for l in range(lat_count):
                    results[c, l, k // 2 * NLAT : (k // 2 + 1) * NLAT] = pair[l * NLAT : (l + 1) * NLAT]
            for l in range(1, lat_count):
                result_copy(c, l).start()
            if i < here - 1:
                result_copy(c, 0).start()
            else:
                returned[mine] = results[c, lat]
    with scope("wo1"):
        wo_cross[1].wait_recv()
        wo_relay[1].start()
    with scope("retw"):
        def back_from(h):
            @pl.when(h != mine)
            def _():
                landed(returned.at[h], t_recv.at[h])

        each(0, lat_count * here, back_from)
        wo_share.wait_recv()
        for copy in wo_relay:
            copy.wait_recv()
    with scope("final"):
        low = low_lanes(NLAT)
        for p in range(lat_count * here // 2):
            a, b = returned[2 * p].astype(F32), returned[2 * p + 1].astype(F32)
            a_swap, b_swap = swap(a), swap(b)
            for g in range(groups):
                at = slice(g // 2 * NLAT, (g // 2 + 1) * NLAT)
                both = jnp.where(low, a[at], b_swap[at]) if g % 2 == 0 else jnp.where(low, a_swap[at], b[at])
                mix[g * NLAT : (g + 1) * NLAT, p * lanes : (p + 1) * lanes] = both.astype(BF16)
        total = dot(mix[...], w_og[...].reshape(lat_width, lat_width))
        final = (lmid[...].astype(F32) + total).astype(BF16)
        lat_out[...] = final
        lfin[...] = dot(rms_norm(final, g_wlat[...]), w_kvw[...]).astype(BF16)

    with scope("drain"):
        for copy in [wo_share] + wo_cross + wo_relay:
            copy.wait_send()
        for g in range(groups):
            for i in range(3):
                lat_copy(g, i).wait_send()

            def sent(h):
                @pl.when(h != head)
                def _():
                    to_head(g, h, None).wait_send()

                each(1, slots, lambda j: to_head(g, h, j).wait_send())

            each(0, here, sent)

        def answered(c):
            for l in range(1, lat_count):
                result_copy(c, l).wait_send()

            @pl.when(c != head)
            def _():
                result_copy(c, 0).wait_send()

        each(0, here, answered)


def back(query, final, mid, key_vals, tok_out, lat_out):
    width = query.shape[1]
    heads = width // HEAD
    keys = spread_heads(key_vals[:, :width], heads)
    values = spread_heads(key_vals[:, width:], heads)
    scores = dot_nt(keys, query[...]).reshape(heads, NLAT, G)
    peak = jnp.max(scores, axis=1, keepdims=True)
    weights = jnp.exp(scores - peak)
    weights = weights * (1.0 / jnp.sum(weights, axis=1, keepdims=True))
    written = dot_tn(weights.reshape(heads * NLAT, G).astype(BF16), values)
    tok_out[...] = (mid[...].astype(F32) + written).astype(BF16)
    lat_out[...] = final[...]


def local(
    tokens, latents, gain_self, w_qkv_tok, w_o_tok, gain_read, w_kv_read, gain_lat, w_q_read,
    gain_glob, w_qkv_glob, w_o_glob, gain_write, w_q_write, gain_wlat, w_kv_write,
):
    dp_count = lax.axis_size("dp")
    lat_count = lax.axis_size("lat")
    rows, width = tokens.shape
    lat_rows, lat_width = latents.shape
    groups = rows // G
    here = w_qkv_glob.shape[2] // HEAD
    line = lat_count * NLAT
    packs = (groups + 1) // 2
    vmem = pl.BlockSpec(memory_space=pltpu.VMEM)
    hbm = pl.BlockSpec(memory_space=pl.ANY)
    dma = pltpu.SemaphoreType.DMA
    query, final, mid, key_vals = pl.pallas_call(
        functools.partial(kernel, dp_count, lat_count),
        out_shape=(
            jax.ShapeDtypeStruct(tokens.shape, BF16),
            jax.ShapeDtypeStruct(latents.shape, BF16),
            jax.ShapeDtypeStruct(tokens.shape, BF16),
            jax.ShapeDtypeStruct((lat_rows, w_kv_write.shape[1]), BF16),
        ),
        in_specs=[hbm] * 16,
        out_specs=(vmem,) * 4,
        scratch_shapes=[
            pltpu.VMEM(tokens.shape, BF16),
            pltpu.VMEM(latents.shape, BF16),
            pltpu.VMEM((1, width), F32),
            pltpu.VMEM((1, width), F32),
            pltpu.VMEM((1, lat_width), F32),
            pltpu.VMEM((1, lat_width), F32),
            pltpu.VMEM((1, width), F32),
            pltpu.VMEM((1, lat_width), F32),
            pltpu.VMEM(w_qkv_tok.shape, BF16),
            pltpu.VMEM(w_o_tok.shape, BF16),
            pltpu.VMEM(w_kv_read.shape, BF16),
            pltpu.VMEM(w_q_read.shape, BF16),
            pltpu.VMEM(w_qkv_glob.shape, BF16),
            pltpu.VMEM((lat_count,) + w_o_glob.shape, BF16),
            pltpu.VMEM(w_q_write.shape, BF16),
            pltpu.VMEM(w_kv_write.shape, BF16),
            pltpu.VMEM(latents.shape, BF16),
            pltpu.VMEM((G, w_qkv_tok.shape[1]), BF16),
            pltpu.VMEM((G, width), BF16),
            pltpu.VMEM((groups, lat_width // HEAD * NLAT, width), BF16),
            pltpu.VMEM((groups, lat_count, NLAT, lat_width), BF16),
            pltpu.VMEM((groups, here, line * 3 // 2, 2 * HEAD), BF16),
            pltpu.VMEM((groups, dp_count, line * 3 // 2, 2 * HEAD), BF16),
            pltpu.VMEM((here, lat_count, packs * NLAT, 2 * HEAD), BF16),
            pltpu.VMEM((lat_count * here, packs * NLAT, 2 * HEAD), BF16),
            pltpu.VMEM(latents.shape, BF16),
            dma((17 + groups,)),
            dma((groups, 3)),
            dma((groups, lat_count)),
            dma((groups, dp_count)),
            dma((groups, dp_count)),
            dma((here, lat_count)),
            dma((lat_count * here,)),
            dma((5,)),
            dma((5,)),
        ],
        compiler_params=pltpu.CompilerParams(
            collective_id=0, has_side_effects=True, vmem_limit_bytes=67043328
        ),
    )(
        tokens, latents, gain_self[None], w_qkv_tok, w_o_tok, gain_read[None], w_kv_read,
        gain_lat[None], w_q_read, gain_glob[None], w_qkv_glob, w_o_glob, gain_write[None],
        w_q_write, gain_wlat[None], w_kv_write,
    )
    per_group = pl.BlockSpec((G, width), lambda g: (g, 0))
    per_lat = pl.BlockSpec((NLAT, lat_width), lambda g: (g, 0))
    return pl.pallas_call(
        back,
        grid=(groups,),
        out_shape=(
            jax.ShapeDtypeStruct(tokens.shape, BF16),
            jax.ShapeDtypeStruct(latents.shape, BF16),
        ),
        in_specs=[
            per_group,
            per_lat,
            per_group,
            pl.BlockSpec((NLAT, key_vals.shape[1]), lambda g: (g, 0)),
        ],
        out_specs=(per_group, per_lat),
    )(query, final, mid, key_vals)


def solution(mesh):
    rows = P(("dp", "lat"), None)
    whole = P()
    placed = (
        rows, rows, whole, whole, whole, whole, whole, whole, whole, whole,
        P(None, None, "lat"), P("lat", None), whole, whole, whole, whole,
    )
    return jax.shard_map(
        local, mesh=mesh, in_specs=placed, out_specs=(rows, rows), check_vma=False
    )
```

time: 47.7 us -> 39.1 us (0.82)
  Pallas kernels: 46.9 us -> 38.3 us
    pallas_call x1, Pallas kernels: 42.7 us -> 34.1 us  [local(): pl.pallas_call(functools.partial(kernel, dp_count, lat_count), out_shape=...]
where the time goes in v3:
time: 39.1 us; the launch traced here: 38.9 us
  Pallas kernels  38.3 us (98%)
  between operations  0.64 us (2%)
    pallas_call x1, Pallas kernels, local(): pl.pallas_call(functools.partial(kernel, dp_count, lat_count), out_shape=...  34.1 us
    pallas_call x1, Pallas kernels, local(): pl.pallas_call(back, grid=(groups,), out_shape=(jax.ShapeDtypeStruct(toke...  4.15 us

profile of v3, /device:TPU:0, one launch (start us, length us, event | category | flops | bytes accessed | tf_op | source)
XLA Modules:
  0.0 38.9 jit_solution(8940759787135989637)
XLA Ops:
  0.6 34.1 %shard_map.167 = (bf16[768,512]{1,0:T(8,128)(2,1)}, bf16[48,1024]{1,0:T(8,128)(2,1)}, bf16[768,512]{1,0:T(8,128)(2,1)}, bf16[48,1024]{1,0:T(8,128)(2,1)}) custom-call(bf16[768,512]{1,0:T(8,128)(2,1)} %tok_h.1, bf16[48,1024]{1,0:T(8,128)(2,1)} %lat_h.1, f32[1,512]{1,0:T(1,128)} %bitcast.9, bf16[512,1536]{1,0:T(8,128)(2,1)} %w_qkv_h.1, ...), custom_call_target="tpu_custom_call" | custom-call | tf_op jit(solution)/shard_map/pallas_call | solution.py:477
  34.8 4.2 %shard_map.168 = (bf16[768,512]{1,0:T(8,128)(2,1)}, bf16[48,1024]{1,0:T(8,128)(2,1)}) custom-call(bf16[768,512]{1,0:T(8,128)(2,1)} %get-tuple-element.6.query, bf16[48,1024]{1,0:T(8,128)(2,1)} %get-tuple-element.7.final, bf16[768,512]{1,0:T(8,128)(2,1)} %get-tuple-element.8.mid, bf16[48,1024]{1,0:T(8,128)(2,1)} %get-tuple-element.9.key_vals), custom_call_target="tpu_custom_call" | custom-call | tf_op jit(solution)/shard_map/pallas_call | solution.py:534

commit v4 on v3

--- a/solution.py
+++ b/solution.py
@@ -10,6 +10,9 @@
 HEAD = 64
 G = 256
 NLAT = 16
+WO_EIGHTHS = (1, 1, 2, 4)
+FRONT_BYTES = 40 * 2**20
+BACK_BYTES = 8 * 2**20
 SCALE = HEAD ** (-0.5)
 LOG2E = 1.4426950408889634
 MESH = pl.DeviceIdType.MESH
@@ -146,14 +149,21 @@
 
     wo_share = remote(w_og_h, w_og.at[lat], wo_send.at[0], wo_recv.at[0], (dp, partner))
     wo_cross, wo_relay = [], []
-    wo_rows = w_og_h.shape[0] // 2
-    for i in range(2):
-        part_rows = pl.ds(i * wo_rows, wo_rows)
+    wo_rows = w_og_h.shape[0] // 8
+    wo_parts = len(WO_EIGHTHS)
+    for i, count in enumerate(WO_EIGHTHS):
+        part_rows = pl.ds(sum(WO_EIGHTHS[:i]) * wo_rows, count * wo_rows)
         there = w_og.at[lat_y, part_rows]
         wo_cross.append(
             remote(w_og_h.at[part_rows], w_og.at[lat, part_rows], wo_send.at[1 + i], wo_recv.at[1 + i], (dp, lat_y))
         )
-        wo_relay.append(remote(there, there, wo_send.at[3 + i], wo_recv.at[3 + i], (dp, partner)))
+        k = 1 + wo_parts + i
+        wo_relay.append(remote(there, there, wo_send.at[k], wo_recv.at[k], (dp, partner)))
+
+    def relay(i):
+        wo_cross[i].wait_recv()
+        wo_relay[i].start()
+
 
     def lat_copy(g, i):
         own = normed_lat.at[g, lat]
@@ -299,17 +309,22 @@
             with scope("bar"):
                 pl.semaphore_wait(barrier, dp_count - 1 + here * (lat_count - 1))
             wo_share.start()
+            wo_cross[0].start()
         with scope(f"read{g}"):
             read_part(g)
+        if g < last:
+            wo_cross[1 + g].start()
         if g == 1:
             later[0].wait()
         if 1 <= g < last:
             with scope(f"proj{g - 1}"):
                 project(g - 1)
-    for copy in wo_cross:
-        copy.start()
+    wo_cross[groups].start()
     with scope("projM"):
         project(last - 1)
+    with scope("rel"):
+        relay(0)
+        relay(1)
     later[1].wait()
     with scope("wq"):
         for g in range(groups):
@@ -323,9 +338,8 @@
     for g in range(last):
         with scope(f"gath{g}"):
             gathered(g)
-    with scope("wo0"):
-        wo_cross[0].wait_recv()
-        wo_relay[0].start()
+    with scope("rel2"):
+        relay(2)
     with scope("gathL"):
         gathered(last)
 
@@ -392,8 +406,7 @@
             else:
                 returned[mine] = results[c, lat]
     with scope("wo1"):
-        wo_cross[1].wait_recv()
-        wo_relay[1].start()
+        relay(3)
     with scope("retw"):
         def back_from(h):
             @pl.when(h != mine)
@@ -445,18 +458,26 @@
         each(0, here, answered)
 
 
-def back(query, final, mid, key_vals, tok_out, lat_out):
+def back(query, final, mid, key_vals, tok_h, lat_h, tok_out, sem):
     width = query.shape[1]
     heads = width // HEAD
-    keys = spread_heads(key_vals[:, :width], heads)
-    values = spread_heads(key_vals[:, width:], heads)
-    scores = dot_nt(keys, query[...]).reshape(heads, NLAT, G)
-    peak = jnp.max(scores, axis=1, keepdims=True)
-    weights = jnp.exp(scores - peak)
-    weights = weights * (1.0 / jnp.sum(weights, axis=1, keepdims=True))
-    written = dot_tn(weights.reshape(heads * NLAT, G).astype(BF16), values)
-    tok_out[...] = (mid[...].astype(F32) + written).astype(BF16)
-    lat_out[...] = final[...]
+    groups = query.shape[0] // G
+    copies = [pltpu.make_async_copy(final, lat_h, sem.at[groups])]
+    copies[0].start()
+    for g in range(groups):
+        rows, lrows = pl.ds(g * G, G), pl.ds(g * NLAT, NLAT)
+        keys = spread_heads(key_vals[lrows, :width], heads)
+        values = spread_heads(key_vals[lrows, width:], heads)
+        scores = dot_nt(keys, query[rows, :]).reshape(heads, NLAT, G)
+        peak = jnp.max(scores, axis=1, keepdims=True)
+        weights = jnp.exp(scores - peak)
+        weights = weights * (1.0 / jnp.sum(weights, axis=1, keepdims=True))
+        written = dot_tn(weights.reshape(heads * NLAT, G).astype(BF16), values)
+        tok_out[rows, :] = (mid[rows, :].astype(F32) + written).astype(BF16)
+        copies.append(pltpu.make_async_copy(tok_out.at[rows], tok_h.at[rows], sem.at[g]))
+        copies[-1].start()
+    for copy in copies:
+        copy.wait()
 
 
 def local(
@@ -472,7 +493,7 @@
     line = lat_count * NLAT
     packs = (groups + 1) // 2
     vmem = pl.BlockSpec(memory_space=pltpu.VMEM)
-    hbm = pl.BlockSpec(memory_space=pl.ANY)
+    hbm = pl.BlockSpec(memory_space=pltpu.HBM)
     dma = pltpu.SemaphoreType.DMA
     query, final, mid, key_vals = pl.pallas_call(
         functools.partial(kernel, dp_count, lat_count),
@@ -518,33 +539,32 @@
             dma((groups, dp_count)),
             dma((here, lat_count)),
             dma((lat_count * here,)),
-            dma((5,)),
-            dma((5,)),
+            dma((1 + 2 * len(WO_EIGHTHS),)),
+            dma((1 + 2 * len(WO_EIGHTHS),)),
         ],
         compiler_params=pltpu.CompilerParams(
-            collective_id=0, has_side_effects=True, vmem_limit_bytes=67043328
+            collective_id=0, has_side_effects=True, vmem_limit_bytes=FRONT_BYTES
         ),
     )(
-        tokens, latents, gain_self[None], w_qkv_tok, w_o_tok, gain_read[None], w_kv_read,
-        gain_lat[None], w_q_read, gain_glob[None], w_qkv_glob, w_o_glob, gain_write[None],
-        w_q_write, gain_wlat[None], w_kv_write,
+        *(
+            pltpu.with_memory_space_constraint(array, pltpu.HBM)
+            for array in (
+                tokens, latents, gain_self[None], w_qkv_tok, w_o_tok, gain_read[None], w_kv_read,
+                gain_lat[None], w_q_read, gain_glob[None], w_qkv_glob, w_o_glob, gain_write[None],
+                w_q_write, gain_wlat[None], w_kv_write,
+            )
+        )
     )
-    per_group = pl.BlockSpec((G, width), lambda g: (g, 0))
-    per_lat = pl.BlockSpec((NLAT, lat_width), lambda g: (g, 0))
     return pl.pallas_call(
         back,
-        grid=(groups,),
         out_shape=(
             jax.ShapeDtypeStruct(tokens.shape, BF16),
             jax.ShapeDtypeStruct(latents.shape, BF16),
         ),
-        in_specs=[
-            per_group,
-            per_lat,
-            per_group,
-            pl.BlockSpec((NLAT, key_vals.shape[1]), lambda g: (g, 0)),
-        ],
-        out_specs=(per_group, per_lat),
+        in_specs=[vmem] * 4,
+        out_specs=(hbm, hbm),
+        scratch_shapes=[pltpu.VMEM(tokens.shape, BF16), dma((groups + 1,))],
+        compiler_params=pltpu.CompilerParams(vmem_limit_bytes=BACK_BYTES),
     )(query, final, mid, key_vals)
 
 

time: 39.1 us -> 36.2 us (0.926)
  Pallas kernels: 38.3 us -> 35.4 us
    pallas_call x1, Pallas kernels: 4.15 us -> 1.9 us  [local(): pl.pallas_call(back, out_shape=(jax.ShapeDtypeStruct(tokens.shape, BF16),...]
    pallas_call x1, Pallas kernels: 34.1 us -> 33.5 us  [local(): pl.pallas_call(functools.partial(kernel, dp_count, lat_count), out_shape=...]
where the time goes in v4:
time: 36.2 us; the launch traced here: 36 us
  Pallas kernels  35.4 us (98%)
  between operations  0.64 us (2%)
    pallas_call x1, Pallas kernels, local(): pl.pallas_call(functools.partial(kernel, dp_count, lat_count), out_shape=...  33.5 us
    pallas_call x1, Pallas kernels, local(): pl.pallas_call(back, out_shape=(jax.ShapeDtypeStruct(tokens.shape, BF16),...  1.9 us

profile of v4, /device:TPU:0, one launch (start us, length us, event | category | flops | bytes accessed | tf_op | source)
XLA Modules:
  0.0 36.0 jit_solution(12362288566876540931)
XLA Ops:
  0.6 33.5 %shard_map.167 = (bf16[768,512]{1,0:T(8,128)(2,1)S(1)}, bf16[48,1024]{1,0:T(8,128)(2,1)S(1)}, bf16[768,512]{1,0:T(8,128)(2,1)S(1)}, bf16[48,1024]{1,0:T(8,128)(2,1)S(1)}) custom-call(bf16[768,512]{1,0:T(8,128)(2,1)} %tok_h.1, bf16[48,1024]{1,0:T(8,128)(2,1)} %lat_h.1, f32[1,512]{1,0:T(1,128)} %bitcast.9, bf16[512,1536]{1,0:T(8,128)(2,1)} %w_qkv_h.1, ...), custom_call_target="tpu_custom_call" | custom-call | tf_op jit(solution)/shard_map/pallas_call | solution.py:498
  34.1 1.9 %shard_map.168 = (bf16[768,512]{1,0:T(8,128)(2,1)}, bf16[48,1024]{1,0:T(8,128)(2,1)}) custom-call(bf16[768,512]{1,0:T(8,128)(2,1)S(1)} %get-tuple-element.6.query, bf16[48,1024]{1,0:T(8,128)(2,1)S(1)} %get-tuple-element.7.final, bf16[768,512]{1,0:T(8,128)(2,1)S(1)} %get-tuple-element.8.mid, bf16[48,1024]{1,0:T(8,128)(2,1)S(1)} %get-tuple-element.9.key_vals), custom_call_target="tpu_custom_call" | custom-call | tf_op jit(solution)/shard_map/pallas_call | solution.py:558

commit v5 on v4

--- a/solution.py
+++ b/solution.py
@@ -66,9 +66,10 @@
     tok_h, lat_h, g_self_h, w_qkv_h, w_o_h, g_read_h, w_kvr_h, g_lat_h, w_qr_h, g_glob_h,
     w_glob_h, w_og_h, g_write_h, w_qw_h, g_wlat_h, w_kvw_h,
     tok_out, lat_out, mid, lfin,
-    tok, lat_in, g_self, g_read, g_lat, g_glob, g_write, g_wlat,
+    tok, lat_in, g_self, g_narrow, g_wide,
     w_qkv, w_o, w_kvr, w_qr, w_glob, w_og, w_qw, w_kvw,
-    lmid, packed, mixed, read_q, normed_lat, outgoing, arrived, results, returned, mix,
+    lmid, packed, mixed, read_q, normed_lat, outgoing, arrived, results, returned,
+    early_q, early_top, early_norm, early_acc,
     load_sem, l_send, l_recv, s_send, s_recv, t_send, t_recv, wo_send, wo_recv,
 ):
     width = tok_h.shape[1]
@@ -88,6 +89,8 @@
     partner = lat + 1 - 2 * core
     diag = (partner + 2) % 4
     upper = head * 2 // here
+    g_read, g_write = g_narrow.at[0], g_narrow.at[1]
+    g_lat, g_glob, g_wlat = g_wide.at[0], g_wide.at[1], g_wide.at[2]
 
     def scope(name):
         return jax.named_scope(name)
@@ -106,6 +109,13 @@
         loads[-1].start()
         return loads[-1]
 
+    def load_all(sources, dst):
+        sem = load_sem.at[len(loads)]
+        for i, src in enumerate(sources):
+            pltpu.make_async_copy(src, dst.at[i], sem).start()
+        loads.append(pltpu.make_async_copy(dst, dst, sem))
+        return loads[-1]
+
     def group_load(g):
         rows = pl.ds(g * G, G)
         return load(tok_h.at[rows], tok.at[rows])
@@ -113,8 +123,7 @@
     tok_load = [group_load(0)]
     gain_load = [load(g_self_h, g_self)]
     qkv_load = []
-    for i in range(3):
-        columns = pl.ds(i * width, width)
+    for columns in (pl.ds(0, width), pl.ds(width, 2 * width)):
         qkv_load.append(load(w_qkv_h.at[:, columns], w_qkv.at[:, columns]))
 
     barrier = pltpu.get_barrier_semaphore()
@@ -127,11 +136,9 @@
         each(0, here, lambda h: greet((h * slots + slot, (lat + o) % lat_count)))
 
     o_load = load(w_o_h, w_o)
-    for src, dst in (
-        (lat_h, lat_in), (g_lat_h, g_lat), (g_read_h, g_read), (g_glob_h, g_glob), (g_write_h, g_write),
-        (g_wlat_h, g_wlat),
-    ):
-        gain_load.append(load(src, dst))
+    gain_load.append(load(lat_h, lat_in))
+    gain_load.append(load_all((g_lat_h, g_glob_h, g_wlat_h), g_wide))
+    gain_load.append(load_all((g_read_h, g_write_h), g_narrow))
     qr_load = load(w_qr_h, w_qr)
     kvr_load = load(w_kvr_h, w_kvr)
     for g in range(1, groups):
@@ -147,18 +154,16 @@
     def landed(ref, sem):
         pltpu.make_async_copy(ref, ref, sem).wait()
 
-    wo_share = remote(w_og_h, w_og.at[lat], wo_send.at[0], wo_recv.at[0], (dp, partner))
+    wo_share = remote(w_og_h, w_og.at[lat], wo_send, wo_recv.at[0], (dp, partner))
     wo_cross, wo_relay = [], []
     wo_rows = w_og_h.shape[0] // 8
-    wo_parts = len(WO_EIGHTHS)
     for i, count in enumerate(WO_EIGHTHS):
         part_rows = pl.ds(sum(WO_EIGHTHS[:i]) * wo_rows, count * wo_rows)
         there = w_og.at[lat_y, part_rows]
         wo_cross.append(
-            remote(w_og_h.at[part_rows], w_og.at[lat, part_rows], wo_send.at[1 + i], wo_recv.at[1 + i], (dp, lat_y))
+            remote(w_og_h.at[part_rows], w_og.at[lat, part_rows], wo_send, wo_recv.at[2 + i], (dp, lat_y))
         )
-        k = 1 + wo_parts + i
-        wo_relay.append(remote(there, there, wo_send.at[k], wo_recv.at[k], (dp, partner)))
+        wo_relay.append(remote(there, there, wo_send, wo_recv.at[1], (dp, partner)))
 
     def relay(i):
         wo_cross[i].wait_recv()
@@ -168,19 +173,21 @@
     def lat_copy(g, i):
         own = normed_lat.at[g, lat]
         peer = (diag, lat_y, partner)[i]
-        return remote(own, own, l_send.at[g, i], l_recv.at[g, lat], (dp, peer))
+        return remote(own, own, l_send, l_recv.at[g], (dp, peer))
 
     def far(i):
         return upper * i + (1 - upper) * (here - 1 - i)
 
     def to_head(g, h, j):
+        src, dst = outgoing.at[g, h], arrived.at[g, dp]
+        if j is None:
+            peer = (h * slots + slot, lat)
+            return remote(src, dst, s_send.at[0], s_recv.at[g, 0], peer)
         rows = pl.ds(0, line)
-        src, dst = outgoing.at[g, h], arrived.at[g, dp]
-        if j is not None:
-            src, dst = src.at[rows], dst.at[rows]
-        spot = 0 if j is None else j
-        peer = (h * slots + (slot + spot) % slots, lat)
-        return remote(src, dst, s_send.at[g, h * slots + spot], s_recv.at[g, dp], peer)
+        peer = (h * slots + (slot + j) % slots, lat)
+        return remote(src.at[rows], dst.at[rows], s_send.at[1], s_recv.at[g, 1], peer)
+
+    full, most = pl.ds(0, here - 1), pl.ds(0, here * (slots - 1))
 
     def spread(g):
         def one(i):
@@ -196,19 +203,9 @@
         arrived[g, dp] = outgoing[g, head]
 
     def gathered(g):
-        def one(h):
-            @pl.when(h != head)
-            def _():
-                source = h * slots + slot
-                landed(arrived.at[g, source], s_recv.at[g, source])
-
-            def other(j):
-                source = h * slots + (slot + j) % slots
-                landed(arrived.at[g, source, pl.ds(0, line)], s_recv.at[g, source])
-
-            each(1, slots, other)
-
-        each(0, here, one)
+        landed(arrived.at[g, full], s_recv.at[g, 0])
+        if slots > 1:
+            landed(arrived.at[g, most, pl.ds(0, line)], s_recv.at[g, 1])
 
     def low_lanes(rows):
         return lax.broadcasted_iota(jnp.int32, (rows, lanes), 1) < HEAD
@@ -217,9 +214,7 @@
         return pltpu.roll(values, HEAD, 1)
 
     def project(g):
-        for i in range(1, lat_count):
-            source = (lat + i) % lat_count
-            landed(normed_lat.at[g, source], l_recv.at[g, source])
+        landed(normed_lat.at[g, pl.ds(0, lat_count - 1)], l_recv.at[g])
         rows = normed_lat[g].reshape(line, lat_width)
         queries = dot(rows, w_glob[0]) * (SCALE * LOG2E)
         keys = dot(rows, w_glob[1])
@@ -247,7 +242,6 @@
         packed[:, :width] = (dot(normed, w_qkv[:, :width]) * (SCALE * LOG2E)).astype(BF16)
         if g == 0:
             qkv_load[1].wait()
-            qkv_load[2].wait()
             for src, dst in (
                 (w_glob_h, w_glob), (w_qw_h, w_qw), (w_kvw_h, w_kvw), (w_og_h, w_og.at[lat]),
             ):
@@ -335,127 +329,151 @@
         project(last)
     later[2].wait()
     later[3].wait()
+    def query_of(c, g):
+        pack = arrived[g, c * slots + slot, line:].astype(F32)
+        low = low_lanes(line // 2)
+        both = (jnp.where(low, pack, 0.0), jnp.where(low, swap(pack), 0.0))
+        return jnp.concatenate(both, axis=0).astype(BF16)
+
+    def key_vals(low, high):
+        return jnp.concatenate(
+            [arrived[g, d, :line] for g in range(low, high) for d in range(dp_count)], axis=0
+        )
+
+    own_at = upper * head + (1 - upper) * (here - 1 - head)
+    order = [far(i + (i + here - own_at) // here) for i in range(here - 1)] + [head]
+    wide = dp_count * line * groups <= 2048
+    batches = [order[i : i + here // 2] for i in range(0, here, here // 2)]
+    early_rows = last * line
+
+    def attend_early(b):
+        query = jnp.concatenate([query_of(c, g) for c in batches[b] for g in range(last)], axis=0)
+        keys = key_vals(0, last)
+        scores = dot_nt(query, keys)
+        peak = jnp.max(scores, axis=-1, keepdims=True)
+        weights = jnp.exp2(scores - peak)
+        early_q[b] = query
+        early_top[b] = peak
+        early_norm[b] = jnp.sum(weights, axis=-1, keepdims=True)
+        early_acc[b] = dot(weights.astype(BF16), keys)
+
+    def attend_late(b):
+        keys = key_vals(last, groups)
+        scores = dot_nt(early_q[b], keys)
+        peak = jnp.maximum(early_top[b], jnp.max(scores, axis=-1, keepdims=True))
+        weights = jnp.exp2(scores - peak)
+        keep = jnp.exp2(early_top[b] - peak)
+        total = early_norm[b] * keep + jnp.sum(weights, axis=-1, keepdims=True)
+        first = (early_acc[b] * keep + dot(weights.astype(BF16), keys)) * (1.0 / total)
+        query = jnp.concatenate([query_of(c, last) for c in batches[b]], axis=0)
+        keys = key_vals(0, groups)
+        second = softmax_mix(query, keys, keys)
+        parts = []
+        for i in range(len(batches[b])):
+            parts.append([first[i * early_rows + g * line : i * early_rows + (g + 1) * line] for g in range(last)])
+            parts[-1].append(second[i * line : (i + 1) * line])
+        return parts
+
+    def attend_long(c):
+        query = jnp.concatenate([query_of(c, g) for g in range(groups)], axis=0)
+
+        def fold(i, carry):
+            peak, total, acc = carry
+            for g in range(groups):
+                keys = arrived[g, i, :line]
+                scores = dot_nt(query, keys)
+                new = jnp.maximum(peak, jnp.max(scores, axis=-1, keepdims=True))
+                weights = jnp.exp2(scores - new)
+                keep = jnp.exp2(peak - new)
+                total = total * keep + jnp.sum(weights, axis=-1, keepdims=True)
+                acc = acc * keep + dot(weights.astype(BF16), keys)
+                peak = new
+            return peak, total, acc
+
+        rows = query.shape[0]
+        start = (
+            jnp.full((rows, 1), -jnp.inf, F32), jnp.zeros((rows, 1), F32), jnp.zeros((rows, lanes), F32)
+        )
+        _, total, acc = lax.fori_loop(0, dp_count, fold, start)
+        out = acc * (1.0 / total)
+        return [out[g * line : (g + 1) * line] for g in range(groups)]
+
+    def result_copy(c, i):
+        to = (lat + i) % lat_count
+        return remote(
+            results.at[c, to], returned.at[head, lat], t_send, t_recv.at[head], (c * slots + slot, to)
+        )
+
+    def answer(c, parts, own):
+        low = low_lanes(line)
+        for k in range(0, groups, 2):
+            even = parts[k]
+            odd = parts[k + 1] if k + 1 < groups else even
+            pair = jnp.where(low, swap(even), odd).astype(BF16)
+            for l in range(lat_count):
+                results[c, l, k // 2 * NLAT : (k // 2 + 1) * NLAT] = pair[l * NLAT : (l + 1) * NLAT]
+        for l in range(1, lat_count):
+            result_copy(c, l).start()
+        if own:
+            returned[head, lat] = results[c, lat]
+        else:
+            result_copy(c, 0).start()
+
     for g in range(last):
         with scope(f"gath{g}"):
             gathered(g)
+    if wide:
+        with scope("attE"):
+            for b in range(len(batches)):
+                attend_early(b)
     with scope("rel2"):
         relay(2)
     with scope("gathL"):
         gathered(last)
-
-    def queries_of(c):
-        parts = []
-        for g in range(groups):
-            pack = arrived[g, c * slots + slot, line:].astype(F32)
-            low = low_lanes(line // 2)
-            parts.append(jnp.where(low, pack, 0.0))
-            parts.append(jnp.where(low, swap(pack), 0.0))
-        return jnp.concatenate(parts, axis=0).astype(BF16)
-
-    def attend(c):
-        query = queries_of(c)
-        if dp_count * line * groups <= 2048:
-            key_vals = jnp.concatenate(
-                [arrived[g, d, :line] for g in range(groups) for d in range(dp_count)], axis=0
-            )
-            return softmax_mix(query, key_vals, key_vals)
-
-        def fold(i, carry):
-            peak, total, acc = carry
-            for g in range(groups):
-                key_vals = arrived[g, i, :line]
-                scores = dot_nt(query, key_vals)
-                new = jnp.maximum(peak, jnp.max(scores, axis=-1, keepdims=True))
-                weights = jnp.exp2(scores - new)
-                keep = jnp.exp2(peak - new)
-                total = total * keep + jnp.sum(weights, axis=-1, keepdims=True)
-                acc = acc * keep + dot(weights.astype(BF16), key_vals)
-                peak = new
-            return peak, total, acc
-
-        rows = query.shape[0]
-        first = (
-            jnp.full((rows, 1), -jnp.inf, F32), jnp.zeros((rows, 1), F32), jnp.zeros((rows, lanes), F32)
-        )
-        _, total, acc = lax.fori_loop(0, dp_count, fold, first)
-        return acc * (1.0 / total)
-
-    mine = lat * here + head
-
-    def result_copy(c, i):
-        to = (lat + i) % lat_count
-        return remote(
-            results.at[c, to], returned.at[mine], t_send.at[c, to], t_recv.at[mine], (c * slots + slot, to)
-        )
-
     with scope("att"):
-        for i in range(here):
-            c = (head + 1 + i) % here
-            out = attend(c)
-            low = low_lanes(line)
-            for k in range(0, groups, 2):
-                even = out[k * line : (k + 1) * line]
-                odd = out[(k + 1) * line : (k + 2) * line] if k + 1 < groups else even
-                pair = jnp.where(low, swap(even), odd).astype(BF16)
-                for l in range(lat_count):
-                    results[c, l, k // 2 * NLAT : (k // 2 + 1) * NLAT] = pair[l * NLAT : (l + 1) * NLAT]
-            for l in range(1, lat_count):
-                result_copy(c, l).start()
-            if i < here - 1:
-                result_copy(c, 0).start()
-            else:
-                returned[mine] = results[c, lat]
+        if wide:
+            for b, batch in enumerate(batches):
+                for c, parts in zip(batch, attend_late(b)):
+                    answer(c, parts, c is head)
+        else:
+            for c in order:
+                answer(c, attend_long(c), c is head)
     with scope("wo1"):
         relay(3)
-    with scope("retw"):
-        def back_from(h):
-            @pl.when(h != mine)
-            def _():
-                landed(returned.at[h], t_recv.at[h])
-
-        each(0, lat_count * here, back_from)
         wo_share.wait_recv()
-        for copy in wo_relay:
-            copy.wait_recv()
-    with scope("final"):
-        low = low_lanes(NLAT)
-        for p in range(lat_count * here // 2):
-            a, b = returned[2 * p].astype(F32), returned[2 * p + 1].astype(F32)
+        landed(w_og.at[0], wo_recv.at[1])
+    total = lmid[...].astype(F32)
+    low = low_lanes(NLAT)
+    for k, h in enumerate([head] + order[-2::-1]):
+        with scope("retw"):
+            landed(returned.at[h, pl.ds(0, lat_count - 1 if k == 0 else lat_count)], t_recv.at[h])
+        tiles = []
+        for p in range(0, lat_count, 2):
+            a, b = returned[h, p].astype(F32), returned[h, p + 1].astype(F32)
             a_swap, b_swap = swap(a), swap(b)
+            column = []
             for g in range(groups):
                 at = slice(g // 2 * NLAT, (g // 2 + 1) * NLAT)
-                both = jnp.where(low, a[at], b_swap[at]) if g % 2 == 0 else jnp.where(low, a_swap[at], b[at])
-                mix[g * NLAT : (g + 1) * NLAT, p * lanes : (p + 1) * lanes] = both.astype(BF16)
-        total = dot(mix[...], w_og[...].reshape(lat_width, lat_width))
-        final = (lmid[...].astype(F32) + total).astype(BF16)
+                column.append(
+                    jnp.where(low, a[at], b_swap[at]) if g % 2 == 0 else jnp.where(low, a_swap[at], b[at])
+                )
+            tiles.append(jnp.concatenate(column, axis=0))
+        rows = pl.ds(pl.multiple_of(h * HEAD, HEAD), HEAD)
+        weights = jnp.concatenate([w_og[l, rows, :] for l in range(lat_count)], axis=0)
+        total = total + dot(jnp.concatenate(tiles, axis=1).astype(BF16), weights)
+    with scope("final"):
+        final = total.astype(BF16)
         lat_out[...] = final
         lfin[...] = dot(rms_norm(final, g_wlat[...]), w_kvw[...]).astype(BF16)
 
     with scope("drain"):
-        for copy in [wo_share] + wo_cross + wo_relay:
-            copy.wait_send()
-        for g in range(groups):
-            for i in range(3):
-                lat_copy(g, i).wait_send()
-
-            def sent(h):
-                @pl.when(h != head)
-                def _():
-                    to_head(g, h, None).wait_send()
-
-                each(1, slots, lambda j: to_head(g, h, j).wait_send())
-
-            each(0, here, sent)
-
-        def answered(c):
-            for l in range(1, lat_count):
-                result_copy(c, l).wait_send()
-
-            @pl.when(c != head)
-            def _():
-                result_copy(c, 0).wait_send()
-
-        each(0, here, answered)
+        landed(w_og.at[pl.ds(0, 3)], wo_send)
+        landed(normed_lat.at[:, pl.ds(0, 3)], l_send)
+        landed(outgoing.at[:, full], s_send.at[0])
+        if slots > 1:
+            landed(arrived.at[:, most, pl.ds(0, line)], s_send.at[1])
+        landed(returned.at[pl.ds(0, here - 1)], t_send)
+        landed(returned.at[0, pl.ds(0, lat_count - 1)], t_send)
 
 
 def back(query, final, mid, key_vals, tok_h, lat_h, tok_out, sem):
@@ -509,11 +527,8 @@
             pltpu.VMEM(tokens.shape, BF16),
             pltpu.VMEM(latents.shape, BF16),
             pltpu.VMEM((1, width), F32),
-            pltpu.VMEM((1, width), F32),
-            pltpu.VMEM((1, lat_width), F32),
-            pltpu.VMEM((1, lat_width), F32),
-            pltpu.VMEM((1, width), F32),
-            pltpu.VMEM((1, lat_width), F32),
+            pltpu.VMEM((2, 1, width), F32),
+            pltpu.VMEM((3, 1, lat_width), F32),
             pltpu.VMEM(w_qkv_tok.shape, BF16),
             pltpu.VMEM(w_o_tok.shape, BF16),
             pltpu.VMEM(w_kv_read.shape, BF16),
@@ -530,17 +545,20 @@
             pltpu.VMEM((groups, here, line * 3 // 2, 2 * HEAD), BF16),
             pltpu.VMEM((groups, dp_count, line * 3 // 2, 2 * HEAD), BF16),
             pltpu.VMEM((here, lat_count, packs * NLAT, 2 * HEAD), BF16),
-            pltpu.VMEM((lat_count * here, packs * NLAT, 2 * HEAD), BF16),
-            pltpu.VMEM(latents.shape, BF16),
-            dma((17 + groups,)),
-            dma((groups, 3)),
-            dma((groups, lat_count)),
-            dma((groups, dp_count)),
-            dma((groups, dp_count)),
-            dma((here, lat_count)),
-            dma((lat_count * here,)),
-            dma((1 + 2 * len(WO_EIGHTHS),)),
-            dma((1 + 2 * len(WO_EIGHTHS),)),
+            pltpu.VMEM((here, lat_count, packs * NLAT, 2 * HEAD), BF16),
+            pltpu.VMEM((2, here // 2 * (groups - 1) * line, 2 * HEAD), BF16),
+            pltpu.VMEM((2, here // 2 * (groups - 1) * line, 1), F32),
+            pltpu.VMEM((2, here // 2 * (groups - 1) * line, 1), F32),
+            pltpu.VMEM((2, here // 2 * (groups - 1) * line, 2 * HEAD), F32),
+            dma((13 + groups,)),
+            dma,
+            dma((groups,)),
+            dma((2,)),
+            dma((groups, 2)),
+            dma,
+            dma((here,)),
+            dma,
+            dma((2 + len(WO_EIGHTHS),)),
         ],
         compiler_params=pltpu.CompilerParams(
             collective_id=0, has_side_effects=True, vmem_limit_bytes=FRONT_BYTES

time: 36.2 us -> 34.8 us (0.961)
  Pallas kernels: 35.4 us -> 33.9 us
    pallas_call x1, Pallas kernels: 33.5 us -> 32 us  [local(): pl.pallas_call(functools.partial(kernel, dp_count, lat_count), out_shape=...]
where the time goes in v5:
time: 34.8 us; the launch traced here: 34.7 us
  Pallas kernels  33.9 us (97%)
  between operations  0.81 us (2%)
    pallas_call x1, Pallas kernels, local(): pl.pallas_call(functools.partial(kernel, dp_count, lat_count), out_shape=...  32 us
    pallas_call x1, Pallas kernels, local(): pl.pallas_call(back, out_shape=(jax.ShapeDtypeStruct(tokens.shape, BF16),...  1.9 us

profile of v5, /device:TPU:0, one launch (start us, length us, event | category | flops | bytes accessed | tf_op | source)
XLA Modules:
  0.0 34.7 jit_solution(13952851321471194808)
XLA Ops:
  0.6 32.0 %shard_map.167 = (bf16[768,512]{1,0:T(8,128)(2,1)S(1)}, bf16[48,1024]{1,0:T(8,128)(2,1)S(1)}, bf16[768,512]{1,0:T(8,128)(2,1)S(1)}, bf16[48,1024]{1,0:T(8,128)(2,1)S(1)}) custom-call(bf16[768,512]{1,0:T(8,128)(2,1)} %tok_h.1, bf16[48,1024]{1,0:T(8,128)(2,1)} %lat_h.1, f32[1,512]{1,0:T(1,128)} %bitcast.9, bf16[512,1536]{1,0:T(8,128)(2,1)} %w_qkv_h.1, ...), custom_call_target="tpu_custom_call" | custom-call | tf_op jit(solution)/shard_map/pallas_call | solution.py:516
  32.6 1.9 %shard_map.168 = (bf16[768,512]{1,0:T(8,128)(2,1)}, bf16[48,1024]{1,0:T(8,128)(2,1)}) custom-call(bf16[768,512]{1,0:T(8,128)(2,1)S(1)} %get-tuple-element.6.query, bf16[48,1024]{1,0:T(8,128)(2,1)S(1)} %get-tuple-element.7.final, bf16[768,512]{1,0:T(8,128)(2,1)S(1)} %get-tuple-element.8.mid, bf16[48,1024]{1,0:T(8,128)(2,1)S(1)} %get-tuple-element.9.key_vals), custom_call_target="tpu_custom_call" | custom-call | tf_op jit(solution)/shard_map/pallas_call | solution.py:576

commit v6 on v5

--- a/solution.py
+++ b/solution.py
@@ -10,7 +10,7 @@
 HEAD = 64
 G = 256
 NLAT = 16
-WO_EIGHTHS = (1, 1, 2, 4)
+WO_EIGHTHS = (1, 1, 1, 5)
 FRONT_BYTES = 40 * 2**20
 BACK_BYTES = 8 * 2**20
 SCALE = HEAD ** (-0.5)
@@ -54,7 +54,10 @@
 
 
 def softmax_mix(stacked, keys, values):
-    scores = dot_nt(stacked, keys)
+    return mix_values(dot_nt(stacked, keys), values)
+
+
+def mix_values(scores, values):
     peak = jnp.max(scores, axis=-1, keepdims=True)
     weights = jnp.exp2(scores - peak)
     total = jnp.sum(weights, axis=-1, keepdims=True)
@@ -88,7 +91,8 @@
     lat_y = (lat + 2) % 4
     partner = lat + 1 - 2 * core
     diag = (partner + 2) % 4
-    upper = head * 2 // here
+    offsets = sorted(range(1, here), key=lambda o: -min(o, here - o)) + [0]
+    order = [(head + o) % here for o in offsets[:-1]] + [head]
     g_read, g_write = g_narrow.at[0], g_narrow.at[1]
     g_lat, g_glob, g_wlat = g_wide.at[0], g_wide.at[1], g_wide.at[2]
 
@@ -175,9 +179,6 @@
         peer = (diag, lat_y, partner)[i]
         return remote(own, own, l_send, l_recv.at[g], (dp, peer))
 
-    def far(i):
-        return upper * i + (1 - upper) * (here - 1 - i)
-
     def to_head(g, h, j):
         src, dst = outgoing.at[g, h], arrived.at[g, dp]
         if j is None:
@@ -190,16 +191,11 @@
     full, most = pl.ds(0, here - 1), pl.ds(0, here * (slots - 1))
 
     def spread(g):
-        def one(i):
-            h = far(i)
-
-            @pl.when(h != head)
-            def _():
-                to_head(g, h, None).start()
-
+        for h in order[:-1]:
             each(1, slots, lambda j: to_head(g, h, j).start())
-
-        each(0, here, one)
+        each(1, slots, lambda j: to_head(g, head, j).start())
+        for h in order[:-1]:
+            to_head(g, h, None).start()
         arrived[g, dp] = outgoing[g, head]
 
     def gathered(g):
@@ -230,7 +226,7 @@
             outgoing[g, h + 1, line:] = jnp.where(low[:half], q_swap[:half], q[half:]).astype(BF16)
         spread(g)
 
-    def self_part(g):
+    def self_part(g, between):
         rows = pl.ds(g * G, G)
         tok_load[g].wait()
         if g == 0:
@@ -247,6 +243,7 @@
             ):
                 later.append(load(src, dst))
         packed[:, width:] = dot(normed, w_qkv[:, width:]).astype(BF16)
+        between(g)
         for pair in range(width // lanes):
             at = pair * lanes
             query = packed[:, at : at + lanes]
@@ -296,9 +293,16 @@
         for i in range(3):
             lat_copy(g, i).start()
 
+    def between(g):
+        if g == 2:
+            later[0].wait()
+        if g >= 2:
+            with scope(f"proj{g - 2}"):
+                project(g - 2)
+
     for g in range(groups):
         with scope(f"self{g}"):
-            self_part(g)
+            self_part(g, between)
         if g == 0:
             with scope("bar"):
                 pl.semaphore_wait(barrier, dp_count - 1 + here * (lat_count - 1))
@@ -308,23 +312,18 @@
             read_part(g)
         if g < last:
             wo_cross[1 + g].start()
-        if g == 1:
-            later[0].wait()
-        if 1 <= g < last:
-            with scope(f"proj{g - 1}"):
-                project(g - 1)
-    wo_cross[groups].start()
     with scope("projM"):
         project(last - 1)
-    with scope("rel"):
-        relay(0)
-        relay(1)
     later[1].wait()
     with scope("wq"):
         for g in range(groups):
             rows = pl.ds(g * G, G)
             query = dot(rms_norm(mid[rows, :], g_write[...]), w_qw[...]).astype(BF16)
             tok_out[rows, :] = query * jnp.asarray(SCALE, BF16)
+    with scope("rel"):
+        relay(0)
+        relay(1)
+        wo_cross[groups].start()
     with scope("projL"):
         project(last)
     later[2].wait()
@@ -340,8 +339,6 @@
             [arrived[g, d, :line] for g in range(low, high) for d in range(dp_count)], axis=0
         )
 
-    own_at = upper * head + (1 - upper) * (here - 1 - head)
-    order = [far(i + (i + here - own_at) // here) for i in range(here - 1)] + [head]
     wide = dp_count * line * groups <= 2048
     batches = [order[i : i + here // 2] for i in range(0, here, here // 2)]
     early_rows = last * line
@@ -357,17 +354,19 @@
         early_norm[b] = jnp.sum(weights, axis=-1, keepdims=True)
         early_acc[b] = dot(weights.astype(BF16), keys)
 
-    def attend_late(b):
-        keys = key_vals(last, groups)
-        scores = dot_nt(early_q[b], keys)
-        peak = jnp.maximum(early_top[b], jnp.max(scores, axis=-1, keepdims=True))
-        weights = jnp.exp2(scores - peak)
+    def late_scores(b):
+        first = dot_nt(early_q[b], key_vals(last, groups))
+        query = jnp.concatenate([query_of(c, last) for c in batches[b]], axis=0)
+        return first, dot_nt(query, key_vals(0, groups))
+
+    def attend_late(b, scores):
+        peak = jnp.maximum(early_top[b], jnp.max(scores[0], axis=-1, keepdims=True))
+        weights = jnp.exp2(scores[0] - peak)
         keep = jnp.exp2(early_top[b] - peak)
         total = early_norm[b] * keep + jnp.sum(weights, axis=-1, keepdims=True)
-        first = (early_acc[b] * keep + dot(weights.astype(BF16), keys)) * (1.0 / total)
-        query = jnp.concatenate([query_of(c, last) for c in batches[b]], axis=0)
-        keys = key_vals(0, groups)
-        second = softmax_mix(query, keys, keys)
+        first = dot(weights.astype(BF16), key_vals(last, groups))
+        first = (early_acc[b] * keep + first) * (1.0 / total)
+        second = mix_values(scores[1], key_vals(0, groups))
         parts = []
         for i in range(len(batches[b])):
             parts.append([first[i * early_rows + g * line : i * early_rows + (g + 1) * line] for g in range(last)])
@@ -426,27 +425,29 @@
         with scope("attE"):
             for b in range(len(batches)):
                 attend_early(b)
-    with scope("rel2"):
+    with scope("rel1"):
         relay(2)
     with scope("gathL"):
         gathered(last)
+    with scope("rel2"):
+        relay(3)
     with scope("att"):
         if wide:
+            late = [late_scores(b) for b in range(len(batches))]
             for b, batch in enumerate(batches):
-                for c, parts in zip(batch, attend_late(b)):
+                for c, parts in zip(batch, attend_late(b, late[b])):
                     answer(c, parts, c is head)
         else:
             for c in order:
                 answer(c, attend_long(c), c is head)
     with scope("wo1"):
-        relay(3)
         wo_share.wait_recv()
         landed(w_og.at[0], wo_recv.at[1])
     total = lmid[...].astype(F32)
     low = low_lanes(NLAT)
-    for k, h in enumerate([head] + order[-2::-1]):
+    for h in order:
         with scope("retw"):
-            landed(returned.at[h, pl.ds(0, lat_count - 1 if k == 0 else lat_count)], t_recv.at[h])
+            landed(returned.at[h, pl.ds(0, lat_count - 1 if h is head else lat_count)], t_recv.at[h])
         tiles = []
         for p in range(0, lat_count, 2):
             a, b = returned[h, p].astype(F32), returned[h, p + 1].astype(F32)

time: 34.8 us -> 34.4 us (0.989)
  no operation moved by 1% of the time
where the time goes in v6:
time: 34.4 us; the launch traced here: 34.2 us
  Pallas kernels  33.6 us (98%)
  between operations  0.64 us (2%)
    pallas_call x1, Pallas kernels, local(): pl.pallas_call(functools.partial(kernel, dp_count, lat_count), out_shape=...  31.7 us
    pallas_call x1, Pallas kernels, local(): pl.pallas_call(back, out_shape=(jax.ShapeDtypeStruct(tokens.shape, BF16),...  1.9 us

profile of v6, /device:TPU:0, one launch (start us, length us, event | category | flops | bytes accessed | tf_op | source)
XLA Modules:
  0.0 34.2 jit_solution(17059741825981559330)
XLA Ops:
  0.6 31.7 %shard_map.167 = (bf16[768,512]{1,0:T(8,128)(2,1)S(1)}, bf16[48,1024]{1,0:T(8,128)(2,1)S(1)}, bf16[768,512]{1,0:T(8,128)(2,1)S(1)}, bf16[48,1024]{1,0:T(8,128)(2,1)S(1)}) custom-call(bf16[768,512]{1,0:T(8,128)(2,1)} %tok_h.1, bf16[48,1024]{1,0:T(8,128)(2,1)} %lat_h.1, f32[1,512]{1,0:T(1,128)} %bitcast.9, bf16[512,1536]{1,0:T(8,128)(2,1)} %w_qkv_h.1, ...), custom_call_target="tpu_custom_call" | custom-call | tf_op jit(solution)/shard_map/pallas_call | solution.py:517
  32.3 1.9 %shard_map.168 = (bf16[768,512]{1,0:T(8,128)(2,1)}, bf16[48,1024]{1,0:T(8,128)(2,1)}) custom-call(bf16[768,512]{1,0:T(8,128)(2,1)S(1)} %get-tuple-element.6.query, bf16[48,1024]{1,0:T(8,128)(2,1)S(1)} %get-tuple-element.7.final, bf16[768,512]{1,0:T(8,128)(2,1)S(1)} %get-tuple-element.8.mid, bf16[48,1024]{1,0:T(8,128)(2,1)S(1)} %get-tuple-element.9.key_vals), custom_call_target="tpu_custom_call" | custom-call | tf_op jit(solution)/shard_map/pallas_call | solution.py:577

commit v7 on v6

--- a/solution.py
+++ b/solution.py
@@ -323,9 +323,9 @@
     with scope("rel"):
         relay(0)
         relay(1)
-        wo_cross[groups].start()
     with scope("projL"):
         project(last)
+    wo_cross[groups].start()
     later[2].wait()
     later[3].wait()
     def query_of(c, g):
@@ -406,11 +406,17 @@
     def answer(c, parts, own):
         low = low_lanes(line)
         for k in range(0, groups, 2):
-            even = parts[k]
-            odd = parts[k + 1] if k + 1 < groups else even
-            pair = jnp.where(low, swap(even), odd).astype(BF16)
-            for l in range(lat_count):
-                results[c, l, k // 2 * NLAT : (k // 2 + 1) * NLAT] = pair[l * NLAT : (l + 1) * NLAT]
+            even = swap(parts[k])
+            if k + 1 < groups:
+                pair = jnp.where(low, even, parts[k + 1]).astype(BF16)
+                for l in range(lat_count):
+                    results[c, l, k // 2 * NLAT : (k // 2 + 1) * NLAT] = pair[l * NLAT : (l + 1) * NLAT]
+            else:
+                for l in range(lat_count):
+                    top = slice(l * NLAT, l * NLAT + NLAT // 2)
+                    bottom = slice(l * NLAT + NLAT // 2, (l + 1) * NLAT)
+                    halves = jnp.where(low[: NLAT // 2], even[top], parts[k][bottom])
+                    results[c, l, k // 2 * NLAT :] = halves.astype(BF16)
         for l in range(1, lat_count):
             result_copy(c, l).start()
         if own:
@@ -429,8 +435,6 @@
         relay(2)
     with scope("gathL"):
         gathered(last)
-    with scope("rel2"):
-        relay(3)
     with scope("att"):
         if wide:
             late = [late_scores(b) for b in range(len(batches))]
@@ -441,23 +445,24 @@
             for c in order:
                 answer(c, attend_long(c), c is head)
     with scope("wo1"):
+        relay(3)
         wo_share.wait_recv()
         landed(w_og.at[0], wo_recv.at[1])
     total = lmid[...].astype(F32)
     low = low_lanes(NLAT)
-    for h in order:
-        with scope("retw"):
+    for k, h in enumerate(order):
+        with scope(f"ret{k}"):
             landed(returned.at[h, pl.ds(0, lat_count - 1 if h is head else lat_count)], t_recv.at[h])
         tiles = []
         for p in range(0, lat_count, 2):
             a, b = returned[h, p].astype(F32), returned[h, p + 1].astype(F32)
             a_swap, b_swap = swap(a), swap(b)
             column = []
-            for g in range(groups):
+            for g in range(0, groups, 2):
                 at = slice(g // 2 * NLAT, (g // 2 + 1) * NLAT)
-                column.append(
-                    jnp.where(low, a[at], b_swap[at]) if g % 2 == 0 else jnp.where(low, a_swap[at], b[at])
-                )
+                mask = low if g + 1 < groups else low[: NLAT // 2]
+                column.append(jnp.where(mask, a[at], b_swap[at]))
+                column.append(jnp.where(mask, a_swap[at], b[at]))
             tiles.append(jnp.concatenate(column, axis=0))
         rows = pl.ds(pl.multiple_of(h * HEAD, HEAD), HEAD)
         weights = jnp.concatenate([w_og[l, rows, :] for l in range(lat_count)], axis=0)
@@ -483,13 +488,15 @@
     groups = query.shape[0] // G
     copies = [pltpu.make_async_copy(final, lat_h, sem.at[groups])]
     copies[0].start()
+    scores = []
     for g in range(groups):
-        rows, lrows = pl.ds(g * G, G), pl.ds(g * NLAT, NLAT)
-        keys = spread_heads(key_vals[lrows, :width], heads)
-        values = spread_heads(key_vals[lrows, width:], heads)
-        scores = dot_nt(keys, query[rows, :]).reshape(heads, NLAT, G)
-        peak = jnp.max(scores, axis=1, keepdims=True)
-        weights = jnp.exp(scores - peak)
+        keys = spread_heads(key_vals[g * NLAT : (g + 1) * NLAT, :width], heads)
+        scores.append(dot_nt(keys, query[g * G : (g + 1) * G, :]).reshape(heads, NLAT, G))
+    for g in range(groups):
+        rows = pl.ds(g * G, G)
+        values = spread_heads(key_vals[g * NLAT : (g + 1) * NLAT, width:], heads)
+        peak = jnp.max(scores[g], axis=1, keepdims=True)
+        weights = jnp.exp(scores[g] - peak)
         weights = weights * (1.0 / jnp.sum(weights, axis=1, keepdims=True))
         written = dot_tn(weights.reshape(heads * NLAT, G).astype(BF16), values)
         tok_out[rows, :] = (mid[rows, :].astype(F32) + written).astype(BF16)
@@ -510,7 +517,6 @@
     groups = rows // G
     here = w_qkv_glob.shape[2] // HEAD
     line = lat_count * NLAT
-    packs = (groups + 1) // 2
     vmem = pl.BlockSpec(memory_space=pltpu.VMEM)
     hbm = pl.BlockSpec(memory_space=pltpu.HBM)
     dma = pltpu.SemaphoreType.DMA
@@ -545,8 +551,8 @@
             pltpu.VMEM((groups, lat_count, NLAT, lat_width), BF16),
             pltpu.VMEM((groups, here, line * 3 // 2, 2 * HEAD), BF16),
             pltpu.VMEM((groups, dp_count, line * 3 // 2, 2 * HEAD), BF16),
-            pltpu.VMEM((here, lat_count, packs * NLAT, 2 * HEAD), BF16),
-            pltpu.VMEM((here, lat_count, packs * NLAT, 2 * HEAD), BF16),
+            pltpu.VMEM((here, lat_count, groups * NLAT // 2, 2 * HEAD), BF16),
+            pltpu.VMEM((here, lat_count, groups * NLAT // 2, 2 * HEAD), BF16),
             pltpu.VMEM((2, here // 2 * (groups - 1) * line, 2 * HEAD), BF16),
             pltpu.VMEM((2, here // 2 * (groups - 1) * line, 1), F32),
             pltpu.VMEM((2, here // 2 * (groups - 1) * line, 1), F32),

time: 34.4 us -> 32.9 us (0.956)
  Pallas kernels: 33.6 us -> 32.1 us
    pallas_call x1, Pallas kernels: 31.7 us -> 30.5 us  [local(): pl.pallas_call(functools.partial(kernel, dp_count, lat_count), out_shape=...]
where the time goes in v7:
time: 32.9 us; the launch traced here: 32.7 us
  Pallas kernels  32.1 us (98%)
  between operations  0.64 us (2%)
    pallas_call x1, Pallas kernels, local(): pl.pallas_call(functools.partial(kernel, dp_count, lat_count), out_shape=...  30.5 us
    pallas_call x1, Pallas kernels, local(): pl.pallas_call(back, out_shape=(jax.ShapeDtypeStruct(tokens.shape, BF16),...  1.56 us

profile of v7, /device:TPU:0, one launch (start us, length us, event | category | flops | bytes accessed | tf_op | source)
XLA Modules:
  0.0 32.7 jit_solution(12153852294357103505)
XLA Ops:
  0.6 30.5 %shard_map.167 = (bf16[768,512]{1,0:T(8,128)(2,1)S(1)}, bf16[48,1024]{1,0:T(8,128)(2,1)S(1)}, bf16[768,512]{1,0:T(8,128)(2,1)S(1)}, bf16[48,1024]{1,0:T(8,128)(2,1)S(1)}) custom-call(bf16[768,512]{1,0:T(8,128)(2,1)} %tok_h.1, bf16[48,1024]{1,0:T(8,128)(2,1)} %lat_h.1, f32[1,512]{1,0:T(1,128)} %bitcast.9, bf16[512,1536]{1,0:T(8,128)(2,1)} %w_qkv_h.1, ...), custom_call_target="tpu_custom_call" | custom-call | tf_op jit(solution)/shard_map/pallas_call | solution.py:523
  31.2 1.6 %shard_map.168 = (bf16[768,512]{1,0:T(8,128)(2,1)}, bf16[48,1024]{1,0:T(8,128)(2,1)}) custom-call(bf16[768,512]{1,0:T(8,128)(2,1)S(1)} %get-tuple-element.6.query, bf16[48,1024]{1,0:T(8,128)(2,1)S(1)} %get-tuple-element.7.final, bf16[768,512]{1,0:T(8,128)(2,1)S(1)} %get-tuple-element.8.mid, bf16[48,1024]{1,0:T(8,128)(2,1)S(1)} %get-tuple-element.9.key_vals), custom_call_target="tpu_custom_call" | custom-call | tf_op jit(solution)/shard_map/pallas_call | solution.py:583

commit v8 on v7

--- a/solution.py
+++ b/solution.py
@@ -10,7 +10,7 @@
 HEAD = 64
 G = 256
 NLAT = 16
-WO_EIGHTHS = (1, 1, 1, 5)
+WO_EIGHTHS = (1, 1, 1, 2, 3)
 FRONT_BYTES = 40 * 2**20
 BACK_BYTES = 8 * 2**20
 SCALE = HEAD ** (-0.5)
@@ -91,8 +91,10 @@
     lat_y = (lat + 2) % 4
     partner = lat + 1 - 2 * core
     diag = (partner + 2) % 4
-    offsets = sorted(range(1, here), key=lambda o: -min(o, here - o)) + [0]
-    order = [(head + o) % here for o in offsets[:-1]] + [head]
+    upper = head * 2 // here
+    own_at = upper * head + (1 - upper) * (here - 1 - head)
+    places = [i + (i + here - own_at) // here for i in range(here - 1)]
+    order = [upper * i + (1 - upper) * (here - 1 - i) for i in places] + [head]
     g_read, g_write = g_narrow.at[0], g_narrow.at[1]
     g_lat, g_glob, g_wlat = g_wide.at[0], g_wide.at[1], g_wide.at[2]
 
@@ -127,8 +129,14 @@
     tok_load = [group_load(0)]
     gain_load = [load(g_self_h, g_self)]
     qkv_load = []
-    for columns in (pl.ds(0, width), pl.ds(width, 2 * width)):
-        qkv_load.append(load(w_qkv_h.at[:, columns], w_qkv.at[:, columns]))
+    for i in range(3):
+        sem = load_sem.at[len(loads)]
+        columns = pl.ds(i * width, width)
+        for k in range(2):
+            rows = pl.ds(k * width // 2, width // 2)
+            pltpu.make_async_copy(w_qkv_h.at[rows, columns], w_qkv.at[rows, columns], sem).start()
+        loads.append(pltpu.make_async_copy(w_qkv.at[:, columns], w_qkv.at[:, columns], sem))
+        qkv_load.append(loads[-1])
 
     barrier = pltpu.get_barrier_semaphore()
 
@@ -191,15 +199,31 @@
     full, most = pl.ds(0, here - 1), pl.ds(0, here * (slots - 1))
 
     def spread(g):
-        for h in order[:-1]:
-            each(1, slots, lambda j: to_head(g, h, j).start())
+        if not staged(g):
+            for h in order[:-1]:
+                each(1, slots, lambda j: to_head(g, h, j).start())
         each(1, slots, lambda j: to_head(g, head, j).start())
         for h in order[:-1]:
             to_head(g, h, None).start()
         arrived[g, dp] = outgoing[g, head]
 
+    def staged(g):
+        return slots > 1 and g < last - 1
+
+    def pass_on(g):
+        landed(arrived.at[g, full], s_recv.at[g, 0])
+        for h in order[:-1]:
+            block = arrived.at[g, h * slots + slot, pl.ds(0, line)]
+
+            def one(j):
+                peer = (head * slots + (slot + j) % slots, lat)
+                remote(block, block, s_send.at[1], s_recv.at[g, 1], peer).start()
+
+            each(1, slots, one)
+
     def gathered(g):
-        landed(arrived.at[g, full], s_recv.at[g, 0])
+        if not staged(g):
+            landed(arrived.at[g, full], s_recv.at[g, 0])
         if slots > 1:
             landed(arrived.at[g, most, pl.ds(0, line)], s_recv.at[g, 1])
 
@@ -238,12 +262,12 @@
         packed[:, :width] = (dot(normed, w_qkv[:, :width]) * (SCALE * LOG2E)).astype(BF16)
         if g == 0:
             qkv_load[1].wait()
+            qkv_load[2].wait()
             for src, dst in (
                 (w_glob_h, w_glob), (w_qw_h, w_qw), (w_kvw_h, w_kvw), (w_og_h, w_og.at[lat]),
             ):
                 later.append(load(src, dst))
         packed[:, width:] = dot(normed, w_qkv[:, width:]).astype(BF16)
-        between(g)
         for pair in range(width // lanes):
             at = pair * lanes
             query = packed[:, at : at + lanes]
@@ -251,6 +275,8 @@
             values = packed[:, 2 * width + at : 2 * width + at + lanes]
             out = softmax_mix(spread_heads(query, 2), keys, values)
             mixed[:, at : at + lanes] = fold_heads(out, 2).astype(BF16)
+            if pair == 1:
+                between(g)
         if g == 0:
             o_load.wait()
         mid[rows, :] = (group.astype(F32) + dot(mixed[...], w_o[...])).astype(BF16)
@@ -321,11 +347,15 @@
             query = dot(rms_norm(mid[rows, :], g_write[...]), w_qw[...]).astype(BF16)
             tok_out[rows, :] = query * jnp.asarray(SCALE, BF16)
     with scope("rel"):
+        for g in range(groups):
+            if staged(g):
+                pass_on(g)
         relay(0)
         relay(1)
+        wo_cross[groups].start()
     with scope("projL"):
         project(last)
-    wo_cross[groups].start()
+    wo_cross[groups + 1].start()
     later[2].wait()
     later[3].wait()
     def query_of(c, g):
@@ -433,6 +463,7 @@
                 attend_early(b)
     with scope("rel1"):
         relay(2)
+        relay(3)
     with scope("gathL"):
         gathered(last)
     with scope("att"):
@@ -445,12 +476,12 @@
             for c in order:
                 answer(c, attend_long(c), c is head)
     with scope("wo1"):
-        relay(3)
+        relay(4)
         wo_share.wait_recv()
         landed(w_og.at[0], wo_recv.at[1])
     total = lmid[...].astype(F32)
     low = low_lanes(NLAT)
-    for k, h in enumerate(order):
+    for k, h in enumerate(order[::-1]):
         with scope(f"ret{k}"):
             landed(returned.at[h, pl.ds(0, lat_count - 1 if h is head else lat_count)], t_recv.at[h])
         tiles = []
@@ -557,7 +588,7 @@
             pltpu.VMEM((2, here // 2 * (groups - 1) * line, 1), F32),
             pltpu.VMEM((2, here // 2 * (groups - 1) * line, 1), F32),
             pltpu.VMEM((2, here // 2 * (groups - 1) * line, 2 * HEAD), F32),
-            dma((13 + groups,)),
+            dma((14 + groups,)),
             dma,
             dma((groups,)),
             dma((2,)),

time: 32.9 us -> 32 us (0.973)
  Pallas kernels: 32.1 us -> 31.2 us
    pallas_call x1, Pallas kernels: 30.5 us -> 29.7 us  [local(): pl.pallas_call(functools.partial(kernel, dp_count, lat_count), out_shape=...]
where the time goes in v8:
time: 32 us; the launch traced here: 31.9 us
  Pallas kernels  31.2 us (98%)
  between operations  0.64 us (2%)
    pallas_call x1, Pallas kernels, local(): pl.pallas_call(functools.partial(kernel, dp_count, lat_count), out_shape=...  29.7 us
    pallas_call x1, Pallas kernels, local(): pl.pallas_call(back, out_shape=(jax.ShapeDtypeStruct(tokens.shape, BF16),...  1.56 us

profile of v8, /device:TPU:0, one launch (start us, length us, event | category | flops | bytes accessed | tf_op | source)
XLA Modules:
  0.0 31.9 jit_solution(17785321849716602942)
XLA Ops:
  0.6 29.7 %shard_map.167 = (bf16[768,512]{1,0:T(8,128)(2,1)S(1)}, bf16[48,1024]{1,0:T(8,128)(2,1)S(1)}, bf16[768,512]{1,0:T(8,128)(2,1)S(1)}, bf16[48,1024]{1,0:T(8,128)(2,1)S(1)}) custom-call(bf16[768,512]{1,0:T(8,128)(2,1)} %tok_h.1, bf16[48,1024]{1,0:T(8,128)(2,1)} %lat_h.1, f32[1,512]{1,0:T(1,128)} %bitcast.9, bf16[512,1536]{1,0:T(8,128)(2,1)} %w_qkv_h.1, ...), custom_call_target="tpu_custom_call" | custom-call | tf_op jit(solution)/shard_map/pallas_call | solution.py:554
  30.3 1.6 %shard_map.168 = (bf16[768,512]{1,0:T(8,128)(2,1)}, bf16[48,1024]{1,0:T(8,128)(2,1)}) custom-call(bf16[768,512]{1,0:T(8,128)(2,1)S(1)} %get-tuple-element.6.query, bf16[48,1024]{1,0:T(8,128)(2,1)S(1)} %get-tuple-element.7.final, bf16[768,512]{1,0:T(8,128)(2,1)S(1)} %get-tuple-element.8.mid, bf16[48,1024]{1,0:T(8,128)(2,1)S(1)} %get-tuple-element.9.key_vals), custom_call_target="tpu_custom_call" | custom-call | tf_op jit(solution)/shard_map/pallas_call | solution.py:614
